TPU v7x, 32 devices: a whole 2x2x4 slice. The times are simulated.
32 devices in a mesh: dp: 16 (over z, y, x), mp: 2 (over core).
Axes of the slice: x: 2, y: 2, z: 4, core: 2. Of those that a mesh axis runs over, the one named last changes fastest.
Arguments:
- tokens: bfloat16 [8192, 1024], P('dp'), may hold values from -6 to 6
- sample_owner: int32 [128], P('dp'), may hold values from 0 to 15, as said below
- sample_slot: int32 [128], P('dp'), may hold values from 0 to 15
- teacher_cache: bfloat16 [256, 64, 3200], P('dp', None, 'mp'), may hold values from -6 to 6
- fc_weight: bfloat16 [1024, 4096], P(None, 'mp'), may hold values from -0.1875 to 0.1875
- proj_weight: bfloat16 [4096, 1024], P('mp'), may hold values from -0.09375 to 0.09375
- head_weight: bfloat16 [1024, 3200], P(None, 'mp'), may hold values from -0.1875 to 0.1875
Outputs:
- fc_grad: float32 [1024, 4096], P('dp', 'mp')
- proj_grad: float32 [4096, 1024], P('mp', 'dp')
- head_grad: float32 [1024, 3200], P('dp', 'mp')
Inputs may be any that keep to these rules, and one draw needn't show every extreme that they name: `sample_owner`: the 8 samples of the index d of dp name 8 different owners, among them (d - 1) mod 16 and (d + 8) mod 16; some owners are named far more often than others.
All inputs are finite; a program needn't handle non-finite values.
Results may differ from a plain program's by a relative error of at most 0.01.
Values may be sent and summed in bfloat16 or wider, within the bound.
A program may use at most 128 MiB of HBM per device.

v0:
```python
import math

import jax
import jax.numpy as jnp
from jax import lax
from jax.sharding import PartitionSpec as P

gelu_coef = 0.7978845608


def normalize(values):
    values = values.astype(jnp.float32)
    center = jnp.mean(values, axis=-1, keepdims=True)
    spread = jnp.mean((values - center) ** 2, axis=-1, keepdims=True)
    inverse = 1.0 / jnp.sqrt(spread + 1e-06)
    return ((values - center) * inverse, inverse)


def gelu_tanh(values):
    return 0.5 * values * (1.0 + jnp.tanh(gelu_coef * (values + 0.044715 * values**3)))


def gelu_slope(values):
    inner = jnp.tanh(gelu_coef * (values + 0.044715 * values**3))
    return 0.5 * (1.0 + inner) + 0.5 * values * (1.0 - inner * inner) * gelu_coef * (
        1.0 + 3.0 * 0.044715 * values * values
    )


def per_device(
    tokens, sample_owner, sample_slot, teacher_cache, fc_weight, proj_weight, head_weight
):
    devices = lax.axis_size("dp")
    tok_rows = tokens.shape[0]
    loss_scale = 1.0 / math.sqrt(tok_rows * devices)
    owner_table = (sample_owner[:, None] == jnp.arange(devices, dtype=jnp.int32)[None, :]).astype(
        jnp.int32
    )
    request = jnp.sum(owner_table * (sample_slot[:, None] + 1), axis=0)
    asked_slots = lax.all_to_all(request, "dp", split_axis=0, concat_axis=0, tiled=True)
    present = asked_slots > 0
    safe_slots = jnp.maximum(asked_slots - 1, 0)
    normal_in, _ = normalize(tokens)
    normed_in = normal_in.astype(jnp.bfloat16)
    pre_act = jnp.dot(normed_in, fc_weight, preferred_element_type=jnp.float32)
    act_out = gelu_tanh(pre_act).astype(jnp.bfloat16)
    partial_value = jnp.dot(act_out, proj_weight, preferred_element_type=jnp.float32)
    mlp_out = lax.psum(partial_value.astype(jnp.bfloat16), "mp").astype(jnp.float32)
    hidden = tokens.astype(jnp.float32) + mlp_out
    normal_out, inverse = normalize(hidden)
    normed_out = normal_out.astype(jnp.bfloat16)
    stored = (
        jnp.take(teacher_cache, safe_slots, axis=0) * present.astype(jnp.bfloat16)[:, None, None]
    )
    arrived = lax.all_to_all(stored, "dp", split_axis=0, concat_axis=0, tiled=True)
    target = jnp.take(arrived, sample_owner, axis=0).reshape(tok_rows, -1)
    pred = jnp.dot(normed_out, head_weight, preferred_element_type=jnp.float32)
    err_scaled = ((pred - target.astype(jnp.float32)) * loss_scale).astype(jnp.bfloat16)
    head_grad = jnp.dot(normed_out.T, err_scaled, preferred_element_type=jnp.float32)
    grad_part = jnp.dot(err_scaled, head_weight.T, preferred_element_type=jnp.float32)
    grad_norm = lax.psum(grad_part.astype(jnp.bfloat16), "mp").astype(jnp.float32)
    grad_hidden = inverse * (
        grad_norm
        - jnp.mean(grad_norm, axis=-1, keepdims=True)
        - normal_out * jnp.mean(grad_norm * normal_out, axis=-1, keepdims=True)
    )
    grad_hidden = grad_hidden.astype(jnp.bfloat16)
    proj_grad = jnp.dot(act_out.T, grad_hidden, preferred_element_type=jnp.float32)
    grad_act = jnp.dot(grad_hidden, proj_weight.T, preferred_element_type=jnp.float32)
    grad_pre = (grad_act * gelu_slope(pre_act)).astype(jnp.bfloat16)
    fc_grad = jnp.dot(normed_in.T, grad_pre, preferred_element_type=jnp.float32)
    fc_shard, proj_shard, head_shard = (
        lax.psum_scatter(fc_grad, "dp", scatter_dimension=0, tiled=True),
        lax.psum_scatter(proj_grad, "dp", scatter_dimension=1, tiled=True),
        lax.psum_scatter(head_grad, "dp", scatter_dimension=0, tiled=True),
    )
    return (fc_shard, proj_shard, head_shard)


def solution(mesh):
    in_specs = (
        P("dp", None),
        P("dp"),
        P("dp"),
        P("dp", None, "mp"),
        P(None, "mp"),
        P("mp", None),
        P(None, "mp"),
    )
    out_specs = (P("dp", "mp"), P("mp", "dp"), P("dp", "mp"))
    return jax.shard_map(
        per_device, mesh=mesh, in_specs=in_specs, out_specs=out_specs, check_vma=False
    )
```

profile of v0, /device:TPU:0, one launch (start us, length us, event | category | flops | bytes accessed | tf_op | source)
XLA Modules:
  0.0 670.2 jit_solution(7344679534830181444)
XLA Ops:
  7.2 0.0 copy-start
  7.2 0.8 broadcast_add_fusion
  8.0 0.9 select_reduce_fusion
  8.9 0.1 copy.16
  9.0 15.4 %all_to_all.14 = s32[16,1,1]{2,1,0:T(1,128)S(1)} all-to-all(s32[16,1,1]{2,1,0:T(1,128)S(1)} %copy.16), channel_id=1, replica_groups=mesh['dp'=16,'mp'=2] {'dp'}, dimensions={0} | all-to-all | bytes 128 | tf_op jit(solution)/shard_map/all_to_all | solution.py:40
  24.4 0.4 fusion.22
  24.8 0.0 copy-done
  24.8 2.7 gather_fusion
  27.5 0.2 fusion.21
  27.7 0.4 compare_reduce_fusion
  28.1 4.2 select_multiply_fusion
  32.3 4.5 all-to-all-start.1
  36.8 0.0 all-reduce.3.cloned.1.call-start
  36.9 1.4 convert_reduce_fusion.1
  38.3 1.6 fusion.11
  39.9 0.0 copy-start.1
  40.0 5.1 fusion.25
  45.1 2.1 copy-done.5
  47.1 0.0 copy-done.1
  47.1 3.6 convolution_convert_fusion.1
  50.8 0.0 all-reduce.3.cloned.1.call-update
  50.8 0.0 all-reduce.5.cloned.1.call-start
  50.9 0.1 broadcast_in_dim.36
  50.9 0.1 broadcast_in_dim.37
  51.0 20.5 %all-reduce.3.cloned.1.call-done = bf16[512,1024]{1,0:T(8,128)(2,1)} async-done(((bf16[512,1024]{1,0:T(8,128)(2,1)}), bf16[512,1024]{1,0:T(8,128)(2,1)}) %all-reduce.3.cloned.1.call-update) | async-done | bytes 1048592 | tf_op jit(solution)/shard_map/psum | solution.py:48
  71.6 1.9 fusion.18
  73.5 2.0 multiply_reduce_fusion
  75.5 26.2 %all-to-all-done.1 = bf16[16,64,1600]{2,1,0:T(8,128)(2,1)} async-done(((bf16[16,64,1600]{2,1,0:T(8,128)(2,1)}), bf16[16,64,1600]{2,1,0:T(8,128)(2,1)}, u32[]{:S(2)}, u32[]{:S(2)}) %all-to-all-start.1) | async-done | bytes 3276832 | tf_op jit(solution)/shard_map/all_to_all | solution.py:55
  101.7 3.9 gather_fusion.1
  105.6 3.6 copy.17
  109.2 5.4 multiply_convert_fusion.1
  114.7 1.2 copy-done.4
  115.8 3.0 convolution_convert_fusion
  118.9 0.0 all-reduce.5.cloned.1.call-update
  118.9 0.2 reduce-scatter.8.cloned.1.call-start
  119.2 7.3 %fusion.27 = f32[1024,1600]{1,0:T(8,128)} fusion(bf16[512,1600]{0,1:T(8,128)(2,1)} %copy-done.4, bf16[512,1024]{1,0:T(8,128)(2,1)} %all-reduce.3.cloned.1.call-done, bf16[512,1024]{1,0:T(8,128)(2,1)} %param.7, f32[512]{0:T(512)S(1)} %add_rsqrt_fusion, f32[512]{0:T(512)S(1)} %broadcast_multiply_fusion.2), kind=kOutput, calls=%fused_computation.57 | convolution fusion | flops 1680867328 | bytes 10293248 | tf_op jit(solution)/shard_map/dot_general | solution.py:59
  126.5 0.0 reduce-scatter.8.cloned.1.call-update
  126.5 0.0 reduce-scatter.4.cloned.1.call-start
  126.5 21.4 %all-reduce.5.cloned.1.call-done = bf16[512,1024]{1,0:T(8,128)(2,1)} async-done(((bf16[512,1024]{1,0:T(8,128)(2,1)}), bf16[512,1024]{1,0:T(8,128)(2,1)}) %all-reduce.5.cloned.1.call-update) | async-done | bytes 1048592 | tf_op jit(solution)/shard_map/psum | solution.py:61
  147.9 2.8 convert_reduce_fusion
  150.7 14.0 %fusion.23 = f32[1024,2048]{1,0:T(8,128)} fusion(bf16[512,1024]{1,0:T(8,128)(2,1)} %param.7, f32[512]{0:T(512)S(1)} %add_rsqrt_fusion.1, f32[512]{0:T(512)S(1)} %broadcast_multiply_fusion.3, f32[512,2048]{1,0:T(8,128)} %copy-done.5, bf16[2048,1024]{1,0:T(8,128)(2,1)} %param.12, bf16[512,1024]{1,0:T(8,128)(2,1)} %all-reduce.5.cloned.1.call-done, ...), kind=kOutput, calls=%fused_computation.55 | convolution fusion | flops 4322754560 | bytes 19935232 | tf_op jit(solution)/shard_map/dot_general | solution.py:71
  164.7 0.0 reduce-scatter.4.cloned.1.call-update
  164.8 0.3 reduce-scatter.6.cloned.1.call-start
  165.0 9.5 %fusion.30 = f32[2048,1024]{0,1:T(8,128)} fusion(f32[512,2048]{1,0:T(8,128)} %copy-done.5, bf16[512,1024]{1,0:T(8,128)(2,1)} %all-reduce.5.cloned.1.call-done, bf16[512,1024]{1,0:T(8,128)(2,1)} %all-reduce.3.cloned.1.call-done, bf16[512,1024]{1,0:T(8,128)(2,1)} %param.7, f32[512]{0:T(512)S(1)} %get-tuple-element.5, f32[512]{0:T(512)S(1)} %get-tuple-element.6, ...), kind=kOutput, calls=%fused_computation.58 | convolution fusion | flops 2162688000 | bytes 15736832 | tf_op jit(solution)/shard_map/dot_general | solution.py:68
  174.5 0.0 reduce-scatter.6.cloned.1.call-update
  174.5 124.0 %reduce-scatter.8.cloned.1.call-done = f32[64,1600]{1,0:T(8,128)} async-done(((f32[1024,1600]{1,0:T(8,128)}), f32[64,1600]{1,0:T(8,128)}) %reduce-scatter.8.cloned.1.call-update) | async-done | bytes 409616 | tf_op jit(solution)/shard_map/reduce_scatter | solution.py:75
  298.5 182.2 %reduce-scatter.4.cloned.1.call-done = f32[64,2048]{1,0:T(8,128)} async-done(((f32[1024,2048]{1,0:T(8,128)}), f32[64,2048]{1,0:T(8,128)}) %reduce-scatter.4.cloned.1.call-update) | async-done | bytes 524304 | tf_op jit(solution)/shard_map/reduce_scatter | solution.py:73
  480.7 183.0 %reduce-scatter.6.cloned.1.call-done = f32[2048,64]{0,1:T(8,128)} async-done(((f32[2048,1024]{0,1:T(8,128)}), f32[2048,64]{0,1:T(8,128)}) %reduce-scatter.6.cloned.1.call-update) | async-done | bytes 524304 | tf_op jit(solution)/shard_map/reduce_scatter | solution.py:74
  (15 shorter events, 0.1 us)
Async XLA Ops:
  7.2 17.7 %copy-start = (bf16[16,64,1600]{2,1,0:T(8,128)(2,1)S(1)}, bf16[16,64,1600]{2,1,0:T(8,128)(2,1)}, u32[]{:S(2)}) copy-start(bf16[16,64,1600]{2,1,0:T(8,128)(2,1)} %param.10) | copy-start | bytes 9830404
  32.3 69.4 %all-to-all-start.1 = ((bf16[16,64,1600]{2,1,0:T(8,128)(2,1)}), bf16[16,64,1600]{2,1,0:T(8,128)(2,1)}, u32[]{:S(2)}, u32[]{:S(2)}) async-start(bf16[16,64,1600]{2,1,0:T(8,128)(2,1)} %select_multiply_fusion), calls=%async_computation.1 | async-start | bytes 6815744 | tf_op jit(solution)/shard_map/all_to_all | solution.py:55
  36.8 34.8 %all-reduce.3.cloned.1.call-start = ((), (), s32[]{:S(2)}) async-start(), calls=%async_computation.5 | async-start | bytes 2097152 | tf_op jit(solution)/shard_map/psum | solution.py:48
  39.9 7.2 %copy-start.1 = (bf16[2048,1024]{1,0:T(8,128)(2,1)S(1)}, bf16[2048,1024]{1,0:T(8,128)(2,1)}, u32[]{:S(2)}) copy-start(bf16[2048,1024]{1,0:T(8,128)(2,1)} %param.12) | copy-start | bytes 12582916
  45.1 2.1 copy-start.5
  47.1 3.7 copy-start.3
  50.8 97.1 %all-reduce.5.cloned.1.call-start = ((), (), s32[]{:S(2)}) async-start(), calls=%async_computation.6 | async-start | bytes 2097152 | tf_op jit(solution)/shard_map/psum | solution.py:61
  109.2 6.6 copy-start.2
  114.7 1.2 copy-start.4
  118.9 179.6 %reduce-scatter.8.cloned.1.call-start = ((), (), s32[]{:S(2)}) async-start(), calls=%async_computation.9 | async-start | bytes 7241728 | tf_op jit(solution)/shard_map/reduce_scatter | solution.py:75
  126.5 354.2 %reduce-scatter.4.cloned.1.call-start = ((), (), s32[]{:S(2)}) async-start(), calls=%async_computation.7 | async-start | bytes 8912896 | tf_op jit(solution)/shard_map/reduce_scatter | solution.py:73
  164.8 498.9 %reduce-scatter.6.cloned.1.call-start = ((), (), s32[]{:S(2)}) async-start(), calls=%async_computation.8 | async-start | bytes 8912896 | tf_op jit(solution)/shard_map/reduce_scatter | solution.py:74
Sparse Core Ops, SparseCore 0:
  50.9 20.6 all-reduce.2
  119.0 28.8 all-reduce.4
  150.8 147.6 reduce-scatter.7
  301.3 179.3 reduce-scatter.3
  483.4 180.2 reduce-scatter.5
where the time goes:
time: 672 us; the launch traced here: 670 us
  waiting for transfers between devices  557 us (83%)
  matrix products  48 us (7%)
  other arithmetic  16.8 us (2%)
  blocking collectives  15.4 us (2%)
  between operations  13.9 us (2%)
  local copies, waits for them, and re-layouts  13.7 us (2%)
    reduce_scatter x1, waiting for transfers between devices, per_device(): lax.psum_scatter(proj_grad, 'dp', scatter_dimension=1, tiled=True)  183 us
    reduce_scatter x1, waiting for transfers between devices, per_device(): lax.psum_scatter(fc_grad, 'dp', scatter_dimension=0, tiled=True)  182 us
    reduce_scatter x1, waiting for transfers between devices, per_device(): lax.psum_scatter(head_grad, 'dp', scatter_dimension=0, tiled=True)  124 us
    all_to_all x1, waiting for transfers between devices, per_device(): lax.all_to_all(stored, 'dp', split_axis=0, concat_axis=0, tiled=True)  26.2 us
    psum x1, waiting for transfers between devices, per_device(): lax.psum(grad_part.astype(jnp.bfloat16), 'mp').astype(jnp.float32)  21.4 us
    psum x1, waiting for transfers between devices, per_device(): lax.psum(partial_value.astype(jnp.bfloat16), 'mp').astype(jnp.float32)  20.5 us
    all_to_all x1, blocking collectives, per_device(): lax.all_to_all(request, 'dp', split_axis=0, concat_axis=0, tiled=True)  15.4 us
    dot_general x1, matrix products, per_device(): fc_grad = jnp.dot(normed_in.T, grad_pre, preferred_element_type=jnp.float32)  14 us
  transfers between devices with their start and end apart: 6, of which 6 were waited for; matrix products, arithmetic and copies ran while one was open for 7% of the time, Pallas kernels for 0%

commit v1 on v0

--- a/solution.py
+++ b/solution.py
@@ -27,6 +27,15 @@
     )
 
 
+def pair_sum(part):
+    size = lax.axis_size("mp")
+    total = part.astype(jnp.float32)
+    for shift in range(1, size):
+        moved = lax.ppermute(part, "mp", [(i, (i + shift) % size) for i in range(size)])
+        total = total + moved.astype(jnp.float32)
+    return total
+
+
 def per_device(
     tokens, sample_owner, sample_slot, teacher_cache, fc_weight, proj_weight, head_weight
 ):
@@ -45,7 +54,7 @@
     pre_act = jnp.dot(normed_in, fc_weight, preferred_element_type=jnp.float32)
     act_out = gelu_tanh(pre_act).astype(jnp.bfloat16)
     partial_value = jnp.dot(act_out, proj_weight, preferred_element_type=jnp.float32)
-    mlp_out = lax.psum(partial_value.astype(jnp.bfloat16), "mp").astype(jnp.float32)
+    mlp_out = pair_sum(partial_value.astype(jnp.bfloat16))
     hidden = tokens.astype(jnp.float32) + mlp_out
     normal_out, inverse = normalize(hidden)
     normed_out = normal_out.astype(jnp.bfloat16)
@@ -58,7 +67,7 @@
     err_scaled = ((pred - target.astype(jnp.float32)) * loss_scale).astype(jnp.bfloat16)
     head_grad = jnp.dot(normed_out.T, err_scaled, preferred_element_type=jnp.float32)
     grad_part = jnp.dot(err_scaled, head_weight.T, preferred_element_type=jnp.float32)
-    grad_norm = lax.psum(grad_part.astype(jnp.bfloat16), "mp").astype(jnp.float32)
+    grad_norm = pair_sum(grad_part.astype(jnp.bfloat16))
     grad_hidden = inverse * (
         grad_norm
         - jnp.mean(grad_norm, axis=-1, keepdims=True)
@@ -70,9 +79,9 @@
     grad_pre = (grad_act * gelu_slope(pre_act)).astype(jnp.bfloat16)
     fc_grad = jnp.dot(normed_in.T, grad_pre, preferred_element_type=jnp.float32)
     fc_shard, proj_shard, head_shard = (
-        lax.psum_scatter(fc_grad, "dp", scatter_dimension=0, tiled=True),
-        lax.psum_scatter(proj_grad, "dp", scatter_dimension=1, tiled=True),
-        lax.psum_scatter(head_grad, "dp", scatter_dimension=0, tiled=True),
+        lax.psum_scatter(fc_grad.astype(jnp.bfloat16), "dp", scatter_dimension=0, tiled=True).astype(jnp.float32),
+        lax.psum_scatter(proj_grad.astype(jnp.bfloat16), "dp", scatter_dimension=1, tiled=True).astype(jnp.float32),
+        lax.psum_scatter(head_grad.astype(jnp.bfloat16), "dp", scatter_dimension=0, tiled=True).astype(jnp.float32),
     )
     return (fc_shard, proj_shard, head_shard)
 

time: 672 us -> 417 us (0.62)
  waiting for transfers between devices: 557 us -> 310 us
  matrix products: 48 us -> 38.1 us
    reduce_scatter x3, waiting for transfers between devices: 489 us -> 258 us  [the longest x1 95.3 us: per_device(): lax.psum_scatter(fc_grad.astype(jnp.bfloat16), 'dp', scatter_dimension=0,...]
    psum x2 -> x0, waiting for transfers between devices: 41.9 us -> none  [the longest x1 21.4 us: per_device(): lax.psum(grad_part.astype(jnp.bfloat16), 'mp').astype(jnp.float32)]
    all_to_all x1, waiting for transfers between devices: 26.2 us -> 46 us  [per_device(): lax.all_to_all(stored, 'dp', split_axis=0, concat_axis=0, tiled=True)]
  transfers between devices with their start and end apart: 6 -> 6, of which waited for: 6 -> 6; matrix products, arithmetic and copies ran while one was open for 7% -> 10% of each run, Pallas kernels for 0% -> 0%
where the time goes in v1:
time: 417 us; the launch traced here: 416 us
  waiting for transfers between devices  310 us (74%)
  matrix products  38.1 us (9%)
  other arithmetic  19.6 us (5%)
  blocking collectives  15.4 us (4%)
  local copies, waits for them, and re-layouts  14.9 us (4%)
  between operations  13.9 us (3%)
  starting transfers between devices  4.86 us (1%)
    reduce_scatter x1, waiting for transfers between devices, per_device(): lax.psum_scatter(fc_grad.astype(jnp.bfloat16), 'dp', scatter_dimension=0,...  95.3 us
    reduce_scatter x1, waiting for transfers between devices, per_device(): lax.psum_scatter(proj_grad.astype(jnp.bfloat16), 'dp', scatter_dimension=...  93.6 us
    reduce_scatter x1, waiting for transfers between devices, per_device(): lax.psum_scatter(head_grad.astype(jnp.bfloat16), 'dp', scatter_dimension=...  69.3 us
    all_to_all x1, waiting for transfers between devices, per_device(): lax.all_to_all(stored, 'dp', split_axis=0, concat_axis=0, tiled=True)  46 us
    all_to_all x1, blocking collectives, per_device(): lax.all_to_all(request, 'dp', split_axis=0, concat_axis=0, tiled=True)  15.4 us
    dot_general x1, matrix products, per_device(): fc_grad = jnp.dot(normed_in.T, grad_pre, preferred_element_type=jnp.float32)  10.7 us
  transfers between devices with their start and end apart: 6, of which 6 were waited for; matrix products, arithmetic and copies ran while one was open for 10% of the time, Pallas kernels for 0%

profile of v1, /device:TPU:0, one launch (start us, length us, event | category | flops | bytes accessed | tf_op | source)
XLA Modules:
  0.0 416.4 jit_solution(3709772999089372527)
XLA Ops:
  7.2 0.0 copy-start
  7.2 0.8 broadcast_add_fusion
  8.0 0.9 select_reduce_fusion
  8.9 0.1 copy.16
  9.0 15.4 %all_to_all.14 = s32[16,1,1]{2,1,0:T(1,128)S(1)} all-to-all(s32[16,1,1]{2,1,0:T(1,128)S(1)} %copy.16), channel_id=1, replica_groups=mesh['dp'=16,'mp'=2] {'dp'}, dimensions={0} | all-to-all | bytes 128 | tf_op jit(solution)/shard_map/all_to_all | solution.py:49
  24.4 0.4 fusion.16
  24.8 2.7 gather_fusion
  27.6 0.4 compare_reduce_fusion
  27.9 0.2 fusion.15
  28.1 4.3 %select_multiply_fusion = bf16[16,64,1600]{2,1,0:T(8,128)(2,1)} fusion(bf16[16,64,1600]{2,1,0:T(8,128)(2,1)} %gather_fusion, pred[16]{0:T(512)(128)(4,1)S(1)} %compare_reduce_fusion, bf16[16]{0:T(256)(128)(2,1)S(1)} %fusion.15), kind=kLoop, calls=%fused_computation.17 | loop fusion | flops 3276800 | bytes 6553648 | tf_op jit(solution)/shard_map/mul | solution.py:62
  32.4 4.5 %all-to-all-start.1 = ((bf16[16,64,1600]{2,1,0:T(8,128)(2,1)}), bf16[16,64,1600]{2,1,0:T(8,128)(2,1)}, u32[]{:S(2)}, u32[]{:S(2)}) async-start(bf16[16,64,1600]{2,1,0:T(8,128)(2,1)} %select_multiply_fusion), calls=%async_computation.1 | async-start | bytes 6815744 | tf_op jit(solution)/shard_map/all_to_all | solution.py:64
  36.9 0.0 reduce-scatter.8.cloned.1.call-start
  37.0 1.4 convert_reduce_fusion
  38.4 1.6 fusion.11
  40.1 5.1 %fusion.18 = f32[512,2048]{1,0:T(8,128)S(1)} fusion(bf16[1024,2048]{1,0:T(8,128)(2,1)} %param.11, bf16[512,1024]{1,0:T(8,128)(2,1)} %param.7, f32[512]{0:T(512)S(1)} %add_rsqrt_fusion.1, f32[512]{0:T(512)S(1)} %broadcast_multiply_fusion.3), kind=kOutput, calls=%fused_computation.53 | convolution fusion | flops 2149580800 | bytes 9441280 | tf_op jit(solution)/shard_map/dot_general | solution.py:54
  45.2 3.7 convolution_convert_fusion.4
  48.9 0.1 broadcast_in_dim.36
  49.0 0.1 broadcast_in_dim.37
  49.1 2.8 collective-permute-done
  51.9 2.3 fusion.22
  54.2 1.3 copy-done.1
  55.5 0.3 multiply_reduce_fusion.1
  55.9 46.0 %all-to-all-done.1 = bf16[16,64,1600]{2,1,0:T(8,128)(2,1)} async-done(((bf16[16,64,1600]{2,1,0:T(8,128)(2,1)}), bf16[16,64,1600]{2,1,0:T(8,128)(2,1)}, u32[]{:S(2)}, u32[]{:S(2)}) %all-to-all-start.1) | async-done | bytes 3276832 | tf_op jit(solution)/shard_map/all_to_all | solution.py:64
  101.8 4.0 gather_fusion.1
  105.8 3.6 copy.17
  109.4 5.4 %multiply_convert_fusion.1 = bf16[512,1600]{0,1:T(8,128)(2,1)S(1)} fusion(bf16[1024,1600]{0,1:T(8,128)(2,1)} %param.13, bf16[512,1600]{0,1:T(8,128)(2,1)} %copy.17, pred[512]{0:T(512)(128)(4,1)S(1)} %broadcast_in_dim.37, f32[512,1024]{1,0:T(8,128)} %copy-done.1, f32[512]{0:T(512)S(1)} %add_rsqrt_fusion, f32[512]{0:T(512)S(1)} %broadcast_multiply_fusion.2), kind=kOutput, calls=%fused_computation.18 | convolution fusion | flops 1683390464 | bytes 8655360 | tf_op jit(solution)/shard_map/dot_general | solution.py:66
  114.8 1.2 copy-done.7
  116.0 4.1 convolution_convert_fusion
  120.1 0.0 reduce-scatter.8.cloned.1.call-update
  120.1 0.2 reduce-scatter.6.cloned.1.call-start
  120.4 4.6 %convolution_convert_fusion.3 = bf16[512,1024]{1,0:T(8,128)(2,1)S(1)} fusion(bf16[512,1600]{0,1:T(8,128)(2,1)} %copy-done.7, bf16[1024,1600]{0,1:T(8,128)(2,1)} %param.13), kind=kOutput, calls=%fused_computation.33 | convolution fusion | flops 1678245888 | bytes 5963776 | tf_op jit(solution)/shard_map/dot_general | solution.py:69
  125.0 0.1 collective-permute-start.1
  125.1 2.6 collective-permute-done.1
  127.7 0.8 fusion.13
  128.5 0.7 multiply_convert_fusion.2
  129.3 1.0 copy-done.4
  130.2 0.8 copy-done.9
  131.1 4.6 %convolution_convert_fusion.1 = bf16[2048,1024]{0,1:T(8,128)(2,1)} fusion(bf16[512,1024]{1,0:T(8,128)(2,1)S(1)} %multiply_convert_fusion.2, f32[512,2048]{1,0:T(8,128)S(1)} %copy-done.9), kind=kOutput, calls=%fused_computation.15 | convolution fusion | flops 2159017984 | bytes 9437184 | tf_op jit(solution)/shard_map/dot_general | solution.py:77
  135.6 0.0 reduce-scatter.6.cloned.1.call-update
  135.6 0.0 reduce-scatter.4.cloned.1.call-start
  135.7 10.7 %convolution_convert_fusion.2 = bf16[1024,2048]{1,0:T(8,128)(2,1)} fusion(bf16[512,1024]{1,0:T(8,128)(2,1)} %param.7, f32[512]{0:T(512)S(1)} %add_rsqrt_fusion.1, f32[512]{0:T(512)S(1)} %broadcast_multiply_fusion.3, f32[512,2048]{1,0:T(8,128)} %copy-done.8, bf16[512,1024]{1,0:T(8,128)(2,1)} %copy-done.4, bf16[2048,1024]{1,0:T(8,128)(2,1)} %param.12), kind=kOutput, calls=%fused_computation.16 | convolution fusion | flops 4319084544 | bytes 14684160 | tf_op jit(solution)/shard_map/dot_general | solution.py:80
  146.4 0.0 reduce-scatter.4.cloned.1.call-update
  146.4 69.3 %reduce-scatter.8.cloned.1.call-done = bf16[64,1600]{1,0:T(8,128)(2,1)} async-done(((bf16[1024,1600]{1,0:T(8,128)(2,1)}), bf16[64,1600]{1,0:T(8,128)(2,1)}) %reduce-scatter.8.cloned.1.call-update) | async-done | bytes 204816 | tf_op jit(solution)/shard_map/reduce_scatter | solution.py:84
  215.7 1.7 convert_element_type.83
  217.4 93.6 %reduce-scatter.6.cloned.1.call-done = bf16[2048,64]{0,1:T(8,128)(2,1)} async-done(((bf16[2048,1024]{0,1:T(8,128)(2,1)}), bf16[2048,64]{0,1:T(8,128)(2,1)}) %reduce-scatter.6.cloned.1.call-update) | async-done | bytes 262160 | tf_op jit(solution)/shard_map/reduce_scatter | solution.py:83
  311.0 1.8 convert_element_type.81
  312.8 95.3 %reduce-scatter.4.cloned.1.call-done = bf16[64,2048]{1,0:T(8,128)(2,1)} async-done(((bf16[1024,2048]{1,0:T(8,128)(2,1)}), bf16[64,2048]{1,0:T(8,128)(2,1)}) %reduce-scatter.4.cloned.1.call-update) | async-done | bytes 262160 | tf_op jit(solution)/shard_map/reduce_scatter | solution.py:82
  408.1 1.8 convert_element_type.79
  (25 shorter events, 0.1 us)
Async XLA Ops:
  7.2 17.7 %copy-start = (bf16[16,64,1600]{2,1,0:T(8,128)(2,1)S(1)}, bf16[16,64,1600]{2,1,0:T(8,128)(2,1)}, u32[]{:S(2)}) copy-start(bf16[16,64,1600]{2,1,0:T(8,128)(2,1)} %param.10) | copy-start | bytes 9830404
  32.4 69.4 %all-to-all-start.1 = ((bf16[16,64,1600]{2,1,0:T(8,128)(2,1)}), bf16[16,64,1600]{2,1,0:T(8,128)(2,1)}, u32[]{:S(2)}, u32[]{:S(2)}) async-start(bf16[16,64,1600]{2,1,0:T(8,128)(2,1)} %select_multiply_fusion), calls=%async_computation.1 | async-start | bytes 6815744 | tf_op jit(solution)/shard_map/all_to_all | solution.py:64
  36.9 178.8 %reduce-scatter.8.cloned.1.call-start = ((), (), s32[]{:S(2)}) async-start(), calls=%async_computation.7 | async-start | bytes 3620864 | tf_op jit(solution)/shard_map/reduce_scatter | solution.py:84
  40.1 5.1 %copy-start.5 = (bf16[2048,1024]{1,0:T(8,128)(2,1)S(1)}, bf16[2048,1024]{1,0:T(8,128)(2,1)}, u32[]{:S(2)}) copy-start(bf16[2048,1024]{1,0:T(8,128)(2,1)} %param.12) | copy-start | bytes 12582916
  45.2 3.7 copy-start.8
  45.2 3.7 copy-start.6
  48.9 3.0 collective-permute-start
  54.2 1.3 copy-start.1
  109.4 6.6 %copy-start.2 = (f32[512,1024]{1,0:T(8,128)S(1)}, f32[512,1024]{1,0:T(8,128)}, u32[]{:S(2)}) copy-start(f32[512,1024]{1,0:T(8,128)} %copy-done.1) | copy-start | bytes 6291460
  114.8 1.2 copy-start.7
  120.1 190.9 %reduce-scatter.6.cloned.1.call-start = ((), (), s32[]{:S(2)}) async-start(), calls=%async_computation.6 | async-start | bytes 4456448 | tf_op jit(solution)/shard_map/reduce_scatter | solution.py:83
  120.3 7.4 %copy-start.3 = (f32[512,1024]{1,0:T(8,128)S(1)}, f32[512,1024]{1,0:T(8,128)}, u32[]{:S(2)}) copy-start(f32[512,1024]{1,0:T(8,128)} %copy-done.1) | copy-start | bytes 6291460
  125.0 2.7 collective-permute-start.1
  128.5 2.6 copy-start.9
  129.2 1.0 copy-start.4
  135.6 272.5 %reduce-scatter.4.cloned.1.call-start = ((), (), s32[]{:S(2)}) async-start(), calls=%async_computation.5 | async-start | bytes 4456448 | tf_op jit(solution)/shard_map/reduce_scatter | solution.py:82
Sparse Core Ops, SparseCore 0:
  120.2 95.4 reduce-scatter.7
  218.0 92.9 reduce-scatter.5
  313.3 94.7 reduce-scatter.3

commit v2 on v1

--- a/solution.py
+++ b/solution.py
@@ -1,8 +1,11 @@
+import functools
 import math
 
 import jax
 import jax.numpy as jnp
 from jax import lax
+from jax.experimental import pallas as pl
+from jax.experimental.pallas import tpu as pltpu
 from jax.sharding import PartitionSpec as P
 
 gelu_coef = 0.7978845608
@@ -36,7 +39,215 @@
     return total
 
 
+def dp_factors(mesh):
+    count = mesh.shape["dp"]
+    lead = mesh.devices.reshape(count, -1)[:, 0]
+    spots = [getattr(device, "coords", None) for device in lead]
+    if any(spot is None for spot in spots):
+        return (count,)
+    sizes, stride = [], 1
+    while stride < count:
+        moved = [a for a in range(len(spots[0])) if spots[0][a] != spots[stride][a]]
+        if len(moved) != 1:
+            return (count,)
+        sizes.append(len({spot[moved[0]] for spot in spots}))
+        stride *= sizes[-1]
+    return tuple(reversed(sizes)) if stride == count else (count,)
+
+
+ROWS = 16
+
+
+class Plan:
+    def __init__(self, factors, shapes):
+        self.factors = tuple(factors)
+        self.strides = [math.prod(factors[i + 1 :]) for i in range(len(factors))]
+        live = [a for a in range(len(factors)) if factors[a] > 1]
+        live.sort(key=lambda a: (factors[a], -a))
+        self.orders = [tuple(live)]
+        if len(live) > 1:
+            self.orders.append((live[1], live[0], *live[2:]))
+        self.live = live
+        self.chunks = []
+        for array, (rows, cols) in enumerate(shapes):
+            step = ROWS if rows % ROWS == 0 else rows
+            for start in range(0, rows, step):
+                order = self.orders[len(self.chunks) % len(self.orders)]
+                self.chunks.append((array, start, step, cols, order))
+
+    def scratch(self):
+        shapes = []
+        for _, _, step, cols, order in self.chunks:
+            rest = list(range(len(self.factors)))
+            for axis in order:
+                rest.remove(axis)
+                dims = tuple(self.factors[a] for a in rest)
+                shapes.append(pltpu.VMEM((self.factors[axis] - 1, *dims, step, cols), jnp.bfloat16))
+                shapes.append(pltpu.VMEM((*dims, step, cols), jnp.bfloat16))
+        return shapes
+
+
+def scatter_kernel(plan, arrays, *refs):
+    grads, outs = refs[:arrays], refs[arrays : 2 * arrays]
+    bufs, (own_sem, send_sem, recv_sem) = refs[2 * arrays : -3], refs[-3:]
+    factors, strides = plan.factors, plan.strides
+    me = lax.axis_index("dp")
+    spot = [(me // strides[a]) % factors[a] for a in range(len(factors))]
+    stages = len(plan.live)
+
+    def peer(axis, hop):
+        place = (spot[axis] + hop) % factors[axis]
+        return place, me + (place - spot[axis]) * strides[axis]
+
+    barrier = pltpu.get_barrier_semaphore()
+    total = 0
+    for axis in plan.live:
+        for hop in range(1, factors[axis]):
+            pl.semaphore_signal(
+                barrier,
+                inc=1,
+                device_id={"dp": peer(axis, hop)[1]},
+                device_id_type=pl.DeviceIdType.MESH,
+            )
+            total += 1
+    pl.semaphore_wait(barrier, total)
+
+    base = {axis: 0 for axis in plan.live}
+    count = 0
+    for axis in plan.live:
+        base[axis] = count
+        count += factors[axis] - 1
+
+    def view(chunk, stage, place):
+        array, start, step, _, order = plan.chunks[chunk]
+        axis = order[stage]
+        rest = [a for a in range(len(factors)) if a not in order[:stage]]
+        index = tuple(place if a == axis else slice(None) for a in rest)
+        if stage == 0:
+            return grads[array].at[(*index, pl.ds(start, step))]
+        return buf(chunk, stage - 1)[1].at[index]
+
+    def buf(chunk, stage):
+        at = 2 * (chunk * stages + stage)
+        return bufs[at], bufs[at + 1]
+
+    def own_copy(chunk):
+        axis = plan.chunks[chunk][4][0]
+        return pltpu.make_async_copy(
+            view(chunk, 0, spot[axis]), buf(chunk, 0)[1], own_sem.at[chunk]
+        )
+
+    def sends(chunk, stage):
+        axis = plan.chunks[chunk][4][stage]
+        made = []
+        for hop in range(1, factors[axis]):
+            place, device = peer(axis, hop)
+            made.append(
+                pltpu.make_async_remote_copy(
+                    src_ref=view(chunk, stage, place),
+                    dst_ref=buf(chunk, stage)[0].at[hop - 1],
+                    send_sem=send_sem.at[chunk, base[axis] + hop - 1],
+                    recv_sem=recv_sem.at[chunk, base[axis] + hop - 1],
+                    device_id={"dp": device},
+                    device_id_type=pl.DeviceIdType.MESH,
+                )
+            )
+        return made
+
+    def launch(chunk, stage):
+        for copy in sends(chunk, stage):
+            copy.start()
+        if stage == 0:
+            own_copy(chunk).start()
+
+    def finish(chunk, stage):
+        array, start, step, _, order = plan.chunks[chunk]
+        axis = order[stage]
+        arrived, kept = buf(chunk, stage)
+        if stage == 0:
+            own_copy(chunk).wait()
+        for copy in sends(chunk, stage):
+            copy.wait_recv()
+        rest = [a for a in range(len(factors)) if a not in order[: stage + 1]]
+        dims = [factors[a] for a in rest]
+
+        def add(flat, carry):
+            at, left = [], flat
+            for size in reversed(dims):
+                at.insert(0, left % size)
+                left = left // size
+            at = tuple(at)
+            if stage == 0:
+                value = kept[at].astype(jnp.float32) if at else kept[...].astype(jnp.float32)
+            else:
+                mine, inner = buf(chunk, stage - 1)[1], list(at)
+                before = [a for a in range(len(factors)) if a not in order[:stage]]
+                inner.insert(before.index(axis), spot[axis])
+                value = mine[tuple(inner)].astype(jnp.float32)
+            for hop in range(1, factors[axis]):
+                value = value + arrived[(hop - 1, *at)].astype(jnp.float32)
+            if stage == stages - 1:
+                outs[array][pl.ds(start, step), :] = value.reshape(step, -1)
+            elif at:
+                kept[at] = value.astype(jnp.bfloat16)
+            return carry
+
+        blocks = math.prod(dims)
+        if blocks == 1:
+            add(0, 0)
+        else:
+            lax.fori_loop(0, blocks, add, 0)
+
+    width = len(plan.orders)
+    groups = [
+        range(at, min(at + width, len(plan.chunks))) for at in range(0, len(plan.chunks), width)
+    ]
+    ahead = 2
+    for group in groups[:ahead]:
+        for chunk in group:
+            launch(chunk, 0)
+    for step in range(len(groups) + stages - 1):
+        for stage in range(stages):
+            if 0 <= step - stage < len(groups):
+                for chunk in groups[step - stage]:
+                    finish(chunk, stage)
+                    if stage + 1 < stages:
+                        launch(chunk, stage + 1)
+                if stage == 0 and step + ahead < len(groups):
+                    for chunk in groups[step + ahead]:
+                        launch(chunk, 0)
+    for chunk in range(len(plan.chunks)):
+        for stage in range(stages):
+            for copy in sends(chunk, stage):
+                copy.wait_send()
+
+
+def scatter_sum(factors, grads):
+    count = math.prod(factors)
+    shapes = [(g.shape[0] // count, g.shape[1]) for g in grads]
+    plan = Plan(factors, shapes)
+    hops = sum(factors[a] - 1 for a in plan.live)
+    chunks = len(plan.chunks)
+    views = [g.reshape(*factors, *shape) for g, shape in zip(grads, shapes)]
+    return pl.pallas_call(
+        functools.partial(scatter_kernel, plan, len(grads)),
+        out_shape=[jax.ShapeDtypeStruct(shape, jnp.float32) for shape in shapes],
+        in_specs=[pl.BlockSpec(memory_space=pl.ANY)] * len(grads),
+        out_specs=[pl.BlockSpec(memory_space=pltpu.VMEM)] * len(grads),
+        scratch_shapes=plan.scratch()
+        + [
+            pltpu.SemaphoreType.DMA((chunks,)),
+            pltpu.SemaphoreType.DMA((chunks, hops)),
+            pltpu.SemaphoreType.DMA((chunks, hops)),
+        ],
+        compiler_params=pltpu.CompilerParams(
+            collective_id=0, has_side_effects=True, vmem_limit_bytes=48 * 1024 * 1024
+        ),
+    )(*views)
+
+
 def per_device(
+    factors,
     tokens, sample_owner, sample_slot, teacher_cache, fc_weight, proj_weight, head_weight
 ):
     devices = lax.axis_size("dp")
@@ -74,15 +285,15 @@
         - normal_out * jnp.mean(grad_norm * normal_out, axis=-1, keepdims=True)
     )
     grad_hidden = grad_hidden.astype(jnp.bfloat16)
-    proj_grad = jnp.dot(act_out.T, grad_hidden, preferred_element_type=jnp.float32)
+    proj_grad = jnp.dot(grad_hidden.T, act_out, preferred_element_type=jnp.float32)
     grad_act = jnp.dot(grad_hidden, proj_weight.T, preferred_element_type=jnp.float32)
     grad_pre = (grad_act * gelu_slope(pre_act)).astype(jnp.bfloat16)
     fc_grad = jnp.dot(normed_in.T, grad_pre, preferred_element_type=jnp.float32)
-    fc_shard, proj_shard, head_shard = (
-        lax.psum_scatter(fc_grad.astype(jnp.bfloat16), "dp", scatter_dimension=0, tiled=True).astype(jnp.float32),
-        lax.psum_scatter(proj_grad.astype(jnp.bfloat16), "dp", scatter_dimension=1, tiled=True).astype(jnp.float32),
-        lax.psum_scatter(head_grad.astype(jnp.bfloat16), "dp", scatter_dimension=0, tiled=True).astype(jnp.float32),
-    )
+    head_shard, proj_shard, fc_shard = scatter_sum(
+        factors,
+        [g.astype(jnp.bfloat16) for g in (head_grad, proj_grad, fc_grad)],
+    )
+    proj_shard = proj_shard.T
     return (fc_shard, proj_shard, head_shard)
 
 
@@ -98,5 +309,6 @@
     )
     out_specs = (P("dp", "mp"), P("mp", "dp"), P("dp", "mp"))
     return jax.shard_map(
-        per_device, mesh=mesh, in_specs=in_specs, out_specs=out_specs, check_vma=False
-    )
+        functools.partial(per_device, dp_factors(mesh)),
+        mesh=mesh, in_specs=in_specs, out_specs=out_specs, check_vma=False
+    )

time: 417 us -> 277 us (0.66)
  waiting for transfers between devices: 310 us -> 48.8 us
  Pallas kernels: 0 us -> 129 us
  between operations: 13.9 us -> 0.78 us
  local copies, waits for them, and re-layouts: 14.9 us -> 19.7 us
    reduce_scatter x3 -> x0, waiting for transfers between devices: 258 us -> none  [the longest x1 95.3 us: per_device(): lax.psum_scatter(fc_grad.astype(jnp.bfloat16), 'dp', scatter_dimension=0,...]
    pallas_call x0 -> x1, Pallas kernels: none -> 129 us  [scatter_sum(): pl.pallas_call(functools.partial(scatter_kernel, plan, len(grads)), out_s...]
    convert_element_type x0 -> x1, local copies, waits for them, and re-layouts: none -> 5.48 us  [per_device(): g.astype(jnp.bfloat16)]
    convert_element_type x3 -> x0, other arithmetic: 5.27 us -> none  [the longest x1 1.78 us: per_device(): lax.psum_scatter(proj_grad.astype(jnp.bfloat16), 'dp', scatter_dimension=...]
  transfers between devices with their start and end apart: 6 -> 3, of which waited for: 6 -> 2; matrix products, arithmetic and copies ran while one was open for 10% -> 9% of each run, Pallas kernels for 0% -> 0%
where the time goes in v2:
time: 277 us; the launch traced here: 276 us
  Pallas kernels  129 us (47%)
  waiting for transfers between devices  48.8 us (18%)
  matrix products  38.7 us (14%)
  local copies, waits for them, and re-layouts  19.7 us (7%)
  other arithmetic  19.1 us (7%)
  blocking collectives  15.4 us (6%)
  starting transfers between devices  4.49 us (2%)
    pallas_call x1, Pallas kernels, scatter_sum(): pl.pallas_call(functools.partial(scatter_kernel, plan, len(grads)), out_s...  129 us
    all_to_all x1, waiting for transfers between devices, per_device(): lax.all_to_all(stored, 'dp', split_axis=0, concat_axis=0, tiled=True)  46 us
    all_to_all x1, blocking collectives, per_device(): lax.all_to_all(request, 'dp', split_axis=0, concat_axis=0, tiled=True)  15.4 us
    dot_general x1, matrix products, per_device(): fc_grad = jnp.dot(normed_in.T, grad_pre, preferred_element_type=jnp.float32)  10.6 us
    gather x2, local copies, waits for them, and re-layouts, per_device(): target = jnp.take(arrived, sample_owner, axis=0).reshape(tok_rows, -1)  7.57 us
    dot_general x1, matrix products, per_device(): jnp.dot(grad_hidden.T, act_out, preferred_element_type=jnp.float32)  7.14 us
  transfers between devices with their start and end apart: 3, of which 2 were waited for; matrix products, arithmetic and copies ran while one was open for 9% of the time, Pallas kernels for 0%

profile of v2, /device:TPU:0, one launch (start us, length us, event | category | flops | bytes accessed | tf_op | source)
XLA Modules:
  0.0 276.2 jit_solution(18078907681977567389)
XLA Ops:
  0.6 0.0 copy-start
  0.6 0.8 broadcast_add_fusion
  1.5 0.9 select_reduce_fusion
  2.4 0.1 copy.20
  2.5 15.4 %all_to_all.14 = s32[16,1,1]{2,1,0:T(1,128)S(1)} all-to-all(s32[16,1,1]{2,1,0:T(1,128)S(1)} %copy.20), channel_id=1, replica_groups=mesh['dp'=16,'mp'=2] {'dp'}, dimensions={0} | all-to-all | bytes 128 | tf_op jit(solution)/shard_map/all_to_all | solution.py:260
  17.9 0.4 fusion.16
  18.3 0.0 copy-done
  18.3 2.7 gather_fusion
  21.0 0.2 fusion.15
  21.2 0.4 compare_reduce_fusion
  21.6 4.3 %select_multiply_fusion = bf16[16,64,1600]{2,1,0:T(8,128)(2,1)} fusion(bf16[16,64,1600]{2,1,0:T(8,128)(2,1)} %gather_fusion, pred[16]{0:T(512)(128)(4,1)S(1)} %compare_reduce_fusion, bf16[16]{0:T(256)(128)(2,1)S(1)} %fusion.15), kind=kLoop, calls=%fused_computation.17 | loop fusion | flops 3276800 | bytes 6553648 | tf_op jit(solution)/shard_map/mul | solution.py:273
  25.9 4.5 %all-to-all-start.1 = ((bf16[16,64,1600]{2,1,0:T(8,128)(2,1)}), bf16[16,64,1600]{2,1,0:T(8,128)(2,1)}, u32[]{:S(2)}, u32[]{:S(2)}) async-start(bf16[16,64,1600]{2,1,0:T(8,128)(2,1)} %select_multiply_fusion), calls=%async_computation.1 | async-start | bytes 6815744 | tf_op jit(solution)/shard_map/all_to_all | solution.py:275
  30.4 1.4 convert_reduce_fusion
  31.8 1.6 fusion.11
  33.5 0.0 copy-start.5
  33.5 5.1 %fusion.18 = f32[512,2048]{1,0:T(8,128)S(1)} fusion(bf16[1024,2048]{1,0:T(8,128)(2,1)} %param.11, bf16[512,1024]{1,0:T(8,128)(2,1)} %param.7, f32[512]{0:T(512)S(1)} %add_rsqrt_fusion.1, f32[512]{0:T(512)S(1)} %broadcast_multiply_fusion.3), kind=kOutput, calls=%fused_computation.53 | convolution fusion | flops 2149580800 | bytes 9441280 | tf_op jit(solution)/shard_map/dot_general | solution.py:265
  38.6 0.0 copy-done.5
  38.6 0.0 copy-start.8
  38.6 0.0 copy-start.7
  38.6 3.7 %convolution_convert_fusion.4 = bf16[512,1024]{1,0:T(8,128)(2,1)} fusion(bf16[2048,1024]{1,0:T(8,128)(2,1)S(1)} %copy-done.5, f32[512,2048]{1,0:T(8,128)S(1)} %fusion.18), kind=kOutput, calls=%fused_computation.34 | convolution fusion | flops 2157445120 | bytes 9437184 | tf_op jit(solution)/shard_map/dot_general | solution.py:267
  42.3 0.0 copy-done.8
  42.3 0.0 collective-permute-start
  42.3 0.0 copy-done.7
  42.3 0.1 broadcast_in_dim.36
  42.4 0.1 broadcast_in_dim.37
  42.5 2.8 %collective-permute-done = bf16[512,1024]{1,0:T(8,128)(2,1)} collective-permute-done((bf16[512,1024]{1,0:T(8,128)(2,1)}, bf16[512,1024]{1,0:T(8,128)(2,1)}, u32[]{:S(2)}, u32[]{:S(2)}) %collective-permute-start) | collective-permute-done | bytes 1048608 | tf_op jit(solution)/shard_map/ppermute | solution.py:37
  45.3 2.3 fusion.22
  47.7 1.3 copy-done.2
  48.9 0.3 multiply_reduce_fusion.1
  49.3 46.0 %all-to-all-done.1 = bf16[16,64,1600]{2,1,0:T(8,128)(2,1)} async-done(((bf16[16,64,1600]{2,1,0:T(8,128)(2,1)}), bf16[16,64,1600]{2,1,0:T(8,128)(2,1)}, u32[]{:S(2)}, u32[]{:S(2)}) %all-to-all-start.1) | async-done | bytes 3276832 | tf_op jit(solution)/shard_map/all_to_all | solution.py:275
  95.3 4.0 %gather_fusion.1 = bf16[8,64,1600]{2,1,0:T(8,128)(2,1)} fusion(bf16[16,64,1600]{2,1,0:T(8,128)(2,1)} %all-to-all-done.1, s32[1024]{0:T(1024)S(1)} %pad_clamp_fusion), kind=kCustom, calls=%fused_computation.1 | custom fusion | bytes 3276832 | tf_op jit(solution)/shard_map/jit(_take)/gather | solution.py:276
  99.3 3.6 %copy.21 = bf16[512,1600]{0,1:T(8,128)(2,1)} copy(bf16[512,1600]{1,0:T(8,128)(2,1)} %bitcast.26) | data formatting | bytes 3276800 | tf_op jit(solution)/shard_map/jit(_take)/gather | solution.py:276
  102.9 5.4 %multiply_convert_fusion.1 = bf16[512,1600]{0,1:T(8,128)(2,1)S(1)} fusion(bf16[1024,1600]{0,1:T(8,128)(2,1)} %param.13, bf16[512,1600]{0,1:T(8,128)(2,1)} %copy.21, pred[512]{0:T(512)(128)(4,1)S(1)} %broadcast_in_dim.37, f32[512,1024]{1,0:T(8,128)} %copy-done.2, f32[512]{0:T(512)S(1)} %add_rsqrt_fusion, f32[512]{0:T(512)S(1)} %broadcast_multiply_fusion.2), kind=kOutput, calls=%fused_computation.18 | convolution fusion | flops 1683390464 | bytes 8655360 | tf_op jit(solution)/shard_map/dot_general | solution.py:277
  108.3 0.0 copy-done.6
  108.3 0.0 copy-start.3
  108.3 3.1 %convolution_convert_fusion.3 = bf16[512,1024]{1,0:T(8,128)(2,1)} fusion(bf16[512,1600]{0,1:T(8,128)(2,1)S(1)} %multiply_convert_fusion.1, bf16[1024,1600]{0,1:T(8,128)(2,1)S(1)} %copy-done.6), kind=kOutput, calls=%fused_computation.33 | convolution fusion | flops 1678245888 | bytes 5963776 | tf_op jit(solution)/shard_map/dot_general | solution.py:280
  111.4 0.0 collective-permute-start.1
  111.4 3.7 %convolution_convert_fusion.2 = bf16[1024,1600]{0,1:T(8,128)(2,1)} fusion(bf16[512,1600]{0,1:T(8,128)(2,1)S(1)} %multiply_convert_fusion.1, f32[512,1024]{1,0:T(8,128)S(1)} %copy-done.3, f32[512]{0:T(512)S(1)} %add_rsqrt_fusion, f32[512]{0:T(512)S(1)} %broadcast_multiply_fusion.2), kind=kOutput, calls=%fused_computation.16 | convolution fusion | flops 1680932864 | bytes 7016448 | tf_op jit(solution)/shard_map/dot_general | solution.py:279
  115.1 5.5 %copy.22 = bf16[1024,1600]{1,0:T(8,128)(2,1)} copy(bf16[1024,1600]{0,1:T(8,128)(2,1)} %convolution_convert_fusion.2) | data formatting | bytes 6553600 | tf_op jit(solution)/shard_map/convert_element_type | solution.py:294
  120.6 0.0 collective-permute-done.1
  120.6 3.1 %fusion.13 = (f32[512]{0:T(512)S(1)}, f32[512]{0:T(512)S(1)}) fusion(bf16[512,1024]{1,0:T(8,128)(2,1)} %collective-permute-done.1, bf16[512,1024]{1,0:T(8,128)(2,1)} %convolution_convert_fusion.3, f32[512]{0:T(512)S(1)} %add_rsqrt_fusion, f32[512,1024]{1,0:T(8,128)} %copy-done.2, f32[512]{0:T(512)S(1)} %broadcast_multiply_fusion.2), kind=kLoop, calls=%fused_computation.31 | loop fusion | flops 4193280 | bytes 4202496 | tf_op jit(solution)/shard_map/reduce_sum | solution.py:284
  123.7 3.3 %multiply_convert_fusion.2 = bf16[512,1024]{1,0:T(8,128)(2,1)} fusion(bf16[512,1024]{1,0:T(8,128)(2,1)} %collective-permute-done.1, bf16[512,1024]{1,0:T(8,128)(2,1)} %convolution_convert_fusion.3, f32[512,1024]{1,0:T(8,128)S(1)} %copy-done.4, f32[512]{0:T(512)S(1)} %get-tuple-element.13, f32[512]{0:T(512)S(1)} %get-tuple-element.14, ...), kind=kLoop, calls=%fused_computation.26 | loop fusion | flops 5242880 | bytes 5251072 | tf_op jit(solution)/shard_map/convert_element_type | solution.py:287
  126.9 10.6 %convolution_convert_fusion = bf16[1024,2048]{1,0:T(8,128)(2,1)} fusion(bf16[512,1024]{1,0:T(8,128)(2,1)} %param.7, f32[512]{0:T(512)S(1)} %add_rsqrt_fusion.1, f32[512]{0:T(512)S(1)} %broadcast_multiply_fusion.3, f32[512,2048]{1,0:T(8,128)} %copy-done.8, bf16[512,1024]{1,0:T(8,128)(2,1)} %multiply_convert_fusion.2, bf16[2048,1024]{1,0:T(8,128)(2,1)} %param.12), kind=kOutput, calls=%fused_computation.14 | convolution fusion | flops 4319084544 | bytes 14684160 | tf_op jit(solution)/shard_map/dot_general | solution.py:291
  137.6 7.1 %convolution_convert_fusion.1 = bf16[1024,2048]{1,0:T(8,128)(2,1)} fusion(bf16[512,1024]{1,0:T(8,128)(2,1)} %multiply_convert_fusion.2, f32[512,2048]{1,0:T(8,128)} %copy-done.8), kind=kOutput, calls=%fused_computation.15 | convolution fusion | flops 2159017984 | bytes 9437184 | tf_op jit(solution)/shard_map/dot_general | solution.py:288
  144.7 129.1 %shard_map.94 = (f32[64,1600]{1,0:T(8,128)S(1)}, f32[64,2048]{1,0:T(8,128)S(1)}, f32[64,2048]{1,0:T(8,128)S(1)}) custom-call(bf16[4,2,2,64,1600]{4,3,2,1,0:T(8,128)(2,1)S(1)} %bitcast.24, bf16[4,2,2,64,2048]{4,3,2,1,0:T(8,128)(2,1)} %bitcast.28, bf16[4,2,2,64,2048]{4,3,2,1,0:T(8,128)(2,1)} %bitcast.27), custom_call_target="tpu_custom_call" | custom-call | tf_op jit(solution)/shard_map/pallas_call | solution.py:232
  273.8 0.8 copy.26
  274.6 0.8 copy.27
  275.4 0.8 copy.28
  (16 shorter events, 0.1 us)
Async XLA Ops:
  0.6 17.7 %copy-start = (bf16[16,64,1600]{2,1,0:T(8,128)(2,1)S(1)}, bf16[16,64,1600]{2,1,0:T(8,128)(2,1)}, u32[]{:S(2)}) copy-start(bf16[16,64,1600]{2,1,0:T(8,128)(2,1)} %param.10) | copy-start | bytes 9830404
  25.9 69.4 %all-to-all-start.1 = ((bf16[16,64,1600]{2,1,0:T(8,128)(2,1)}), bf16[16,64,1600]{2,1,0:T(8,128)(2,1)}, u32[]{:S(2)}, u32[]{:S(2)}) async-start(bf16[16,64,1600]{2,1,0:T(8,128)(2,1)} %select_multiply_fusion), calls=%async_computation.1 | async-start | bytes 6815744 | tf_op jit(solution)/shard_map/all_to_all | solution.py:275
  33.5 5.1 %copy-start.5 = (bf16[2048,1024]{1,0:T(8,128)(2,1)S(1)}, bf16[2048,1024]{1,0:T(8,128)(2,1)}, u32[]{:S(2)}) copy-start(bf16[2048,1024]{1,0:T(8,128)(2,1)} %param.12) | copy-start | bytes 12582916
  38.6 3.7 %copy-start.8 = (f32[512,2048]{1,0:T(8,128)}, f32[512,2048]{1,0:T(8,128)S(1)}, u32[]{:S(2)}) copy-start(f32[512,2048]{1,0:T(8,128)S(1)} %fusion.18) | copy-start | bytes 12582916
  38.6 3.7 %copy-start.7 = (s32[8]{0:T(128)S(1)}, s32[8]{0:T(128)}, u32[]{:S(2)}) copy-start(s32[8]{0:T(128)} %param.8) | copy-start | bytes 100
  42.3 3.0 %collective-permute-start = (bf16[512,1024]{1,0:T(8,128)(2,1)}, bf16[512,1024]{1,0:T(8,128)(2,1)}, u32[]{:S(2)}, u32[]{:S(2)}) collective-permute-start(bf16[512,1024]{1,0:T(8,128)(2,1)} %convolution_convert_fusion.4), channel_id=1, source_target_pairs={{0,1},{1,0},{2,3},{3,2},{4,5},{5,4},{6,7},{7,6},{8,9},{9,8},{10,11... | collective-permute-start | bytes 3145736 | tf_op jit(solution)/shard_map/ppermute | solution.py:37
  47.6 1.3 copy-start.2
  102.9 5.4 %copy-start.6 = (bf16[1024,1600]{0,1:T(8,128)(2,1)S(1)}, bf16[1024,1600]{0,1:T(8,128)(2,1)}, u32[]{:S(2)}) copy-start(bf16[1024,1600]{0,1:T(8,128)(2,1)} %param.13) | copy-start | bytes 9830404
  108.3 3.1 %copy-start.3 = (f32[512,1024]{1,0:T(8,128)S(1)}, f32[512,1024]{1,0:T(8,128)}, u32[]{:S(2)}) copy-start(f32[512,1024]{1,0:T(8,128)} %copy-done.2) | copy-start | bytes 6291460
  111.4 9.2 %collective-permute-start.1 = (bf16[512,1024]{1,0:T(8,128)(2,1)}, bf16[512,1024]{1,0:T(8,128)(2,1)}, u32[]{:S(2)}, u32[]{:S(2)}) collective-permute-start(bf16[512,1024]{1,0:T(8,128)(2,1)} %convolution_convert_fusion.3), channel_id=1, source_target_pairs={{0,1},{1,0},{2,3},{3,2},{4,5},{5,4},{6,7},{7,6},{8,9},{9,8},{10,11... | collective-permute-start | bytes 3145736 | tf_op jit(solution)/shard_map/ppermute | solution.py:37
  120.6 3.1 %copy-start.4 = (f32[512,1024]{1,0:T(8,128)S(1)}, f32[512,1024]{1,0:T(8,128)}, u32[]{:S(2)}) copy-start(f32[512,1024]{1,0:T(8,128)} %copy-done.2) | copy-start | bytes 6291460
  137.6 7.1 %copy-start.1 = (bf16[1024,1600]{1,0:T(8,128)(2,1)S(1)}, bf16[1024,1600]{1,0:T(8,128)(2,1)}, u32[]{:S(2)}) copy-start(bf16[1024,1600]{1,0:T(8,128)(2,1)} %copy.22) | copy-start | bytes 9830404

commit v3 on v2

--- a/solution.py
+++ b/solution.py
@@ -69,11 +69,19 @@
             self.orders.append((live[1], live[0], *live[2:]))
         self.live = live
         self.chunks = []
+        early = len(live) > 2 and sum(rows // ROWS for rows, _ in shapes) > 6
         for array, (rows, cols) in enumerate(shapes):
             step = ROWS if rows % ROWS == 0 else rows
             for start in range(0, rows, step):
                 order = self.orders[len(self.chunks) % len(self.orders)]
+                if early and not self.chunks:
+                    order = (live[2], live[1], live[0], *live[3:])
                 self.chunks.append((array, start, step, cols, order))
+        width, rest = len(self.orders), list(range(int(early), len(self.chunks)))
+        self.groups = [rest[at : at + width] for at in range(0, len(rest), width)]
+        self.early = [0] if early else []
+        if early:
+            self.groups[2] = [*self.groups[2], 0]
 
     def scratch(self):
         shapes = []
@@ -198,12 +206,9 @@
         else:
             lax.fori_loop(0, blocks, add, 0)
 
-    width = len(plan.orders)
-    groups = [
-        range(at, min(at + width, len(plan.chunks))) for at in range(0, len(plan.chunks), width)
-    ]
+    groups = plan.groups
     ahead = 2
-    for group in groups[:ahead]:
+    for group in [groups[0], plan.early, *groups[1:ahead]]:
         for chunk in group:
             launch(chunk, 0)
     for step in range(len(groups) + stages - 1):
@@ -215,7 +220,8 @@
                         launch(chunk, stage + 1)
                 if stage == 0 and step + ahead < len(groups):
                     for chunk in groups[step + ahead]:
-                        launch(chunk, 0)
+                        if chunk not in plan.early:
+                            launch(chunk, 0)
     for chunk in range(len(plan.chunks)):
         for stage in range(stages):
             for copy in sends(chunk, stage):
@@ -246,6 +252,60 @@
     )(*views)
 
 
+def error_kernel(scale, owner_ref, pred_ref, block_ref, out_ref):
+    gap = pred_ref[...] - block_ref[...].astype(jnp.float32)
+    out_ref[...] = (gap * scale).astype(out_ref.dtype)
+
+
+def scaled_error(scale, sample_owner, pred, arrived):
+    patches, width = arrived.shape[1:]
+    rows = pl.BlockSpec((patches, width), lambda i, owner: (i, 0))
+    picked = pl.BlockSpec((None, patches, width), lambda i, owner: (owner[i], 0, 0))
+    return pl.pallas_call(
+        functools.partial(error_kernel, scale),
+        out_shape=jax.ShapeDtypeStruct(pred.shape, jnp.bfloat16),
+        grid_spec=pltpu.PrefetchScalarGridSpec(
+            num_scalar_prefetch=1,
+            grid=(sample_owner.shape[0],),
+            in_specs=[rows, picked],
+            out_specs=rows,
+        ),
+        cost_estimate=pl.CostEstimate(
+            flops=2 * pred.size, bytes_accessed=8 * pred.size, transcendentals=0
+        ),
+    )(sample_owner, pred, arrived)
+
+
+def rows_kernel(left_ref, right_ref, out_ref):
+    out_ref[...] = lax.dot_general(
+        left_ref[...],
+        right_ref[...],
+        (((0,), (0,)), ((), ())),
+        preferred_element_type=jnp.float32,
+    ).astype(out_ref.dtype)
+
+
+def outer_product(left, right):
+    depth, rows = left.shape
+    cols = right.shape[1]
+    tile = 256 if rows % 256 == 0 else rows
+    return pl.pallas_call(
+        rows_kernel,
+        out_shape=jax.ShapeDtypeStruct((rows, cols), jnp.bfloat16),
+        grid=(rows // tile,),
+        in_specs=[
+            pl.BlockSpec((depth, tile), lambda i: (0, i)),
+            pl.BlockSpec((depth, cols), lambda i: (0, 0)),
+        ],
+        out_specs=pl.BlockSpec((tile, cols), lambda i: (i, 0)),
+        cost_estimate=pl.CostEstimate(
+            flops=2 * depth * rows * cols,
+            bytes_accessed=2 * (depth * rows + depth * cols + rows * cols),
+            transcendentals=0,
+        ),
+    )(left, right)
+
+
 def per_device(
     factors,
     tokens, sample_owner, sample_slot, teacher_cache, fc_weight, proj_weight, head_weight
@@ -258,7 +318,6 @@
     )
     request = jnp.sum(owner_table * (sample_slot[:, None] + 1), axis=0)
     asked_slots = lax.all_to_all(request, "dp", split_axis=0, concat_axis=0, tiled=True)
-    present = asked_slots > 0
     safe_slots = jnp.maximum(asked_slots - 1, 0)
     normal_in, _ = normalize(tokens)
     normed_in = normal_in.astype(jnp.bfloat16)
@@ -269,14 +328,11 @@
     hidden = tokens.astype(jnp.float32) + mlp_out
     normal_out, inverse = normalize(hidden)
     normed_out = normal_out.astype(jnp.bfloat16)
-    stored = (
-        jnp.take(teacher_cache, safe_slots, axis=0) * present.astype(jnp.bfloat16)[:, None, None]
-    )
+    stored = jnp.take(teacher_cache, safe_slots, axis=0, mode="clip")
     arrived = lax.all_to_all(stored, "dp", split_axis=0, concat_axis=0, tiled=True)
-    target = jnp.take(arrived, sample_owner, axis=0).reshape(tok_rows, -1)
     pred = jnp.dot(normed_out, head_weight, preferred_element_type=jnp.float32)
-    err_scaled = ((pred - target.astype(jnp.float32)) * loss_scale).astype(jnp.bfloat16)
-    head_grad = jnp.dot(normed_out.T, err_scaled, preferred_element_type=jnp.float32)
+    err_scaled = scaled_error(loss_scale, sample_owner, pred, arrived)
+    head_grad = outer_product(normed_out, err_scaled)
     grad_part = jnp.dot(err_scaled, head_weight.T, preferred_element_type=jnp.float32)
     grad_norm = pair_sum(grad_part.astype(jnp.bfloat16))
     grad_hidden = inverse * (

time: 277 us -> 258 us (0.931)
  local copies, waits for them, and re-layouts: 19.7 us -> 6.16 us
  Pallas kernels: 129 us -> 134 us
  other arithmetic: 19.1 us -> 14.2 us
  matrix products: 38.7 us -> 35 us
    pallas_call x0 -> x2, Pallas kernels: none -> 12.7 us  [the longest x1 6.89 us: scaled_error(): pl.pallas_call(functools.partial(error_kernel, scale), out_shape=jax.Shap...]
    pallas_call x1, Pallas kernels: 129 us -> 121 us  [scatter_sum(): pl.pallas_call(functools.partial(scatter_kernel, plan, len(grads)), out_s...]
    gather x3 -> x1, local copies, waits for them, and re-layouts: 10.3 us -> 2.7 us  [per_device(): stored = jnp.take(teacher_cache, safe_slots, axis=0, mode='clip')]
    convert_element_type x1 -> x0, local copies, waits for them, and re-layouts: 5.48 us -> none  [per_device(): g.astype(jnp.bfloat16)]
    mul x2 -> x0, other arithmetic: 4.51 us -> none  [per_device(): jnp.take(teacher_cache, safe_slots, axis=0)]
    dot_general x1 -> x0, matrix products: 3.73 us -> none  [per_device(): jnp.dot(normed_out.T, err_scaled, preferred_element_type=jnp.float32)]
  transfers between devices with their start and end apart: 3 -> 3, of which waited for: 2 -> 2; matrix products, arithmetic and copies ran while one was open for 9% -> 6% of each run, Pallas kernels for 0% -> 2%
where the time goes in v3:
time: 258 us; the launch traced here: 257 us
  Pallas kernels  134 us (52%)
  waiting for transfers between devices  47.2 us (18%)
  matrix products  35 us (14%)
  blocking collectives  15.4 us (6%)
  other arithmetic  14.2 us (6%)
  local copies, waits for them, and re-layouts  6.16 us (2%)
  starting transfers between devices  4.57 us (2%)
    pallas_call x1, Pallas kernels, scatter_sum(): pl.pallas_call(functools.partial(scatter_kernel, plan, len(grads)), out_s...  121 us
    all_to_all x1, waiting for transfers between devices, per_device(): lax.all_to_all(stored, 'dp', split_axis=0, concat_axis=0, tiled=True)  44.6 us
    all_to_all x1, blocking collectives, per_device(): lax.all_to_all(request, 'dp', split_axis=0, concat_axis=0, tiled=True)  15.4 us
    dot_general x1, matrix products, per_device(): fc_grad = jnp.dot(normed_in.T, grad_pre, preferred_element_type=jnp.float32)  10.7 us
    dot_general x1, matrix products, per_device(): jnp.dot(grad_hidden.T, act_out, preferred_element_type=jnp.float32)  7.22 us
    pallas_call x1, Pallas kernels, scaled_error(): pl.pallas_call(functools.partial(error_kernel, scale), out_shape=jax.Shap...  6.89 us
    pallas_call x1, Pallas kernels, outer_product(): pl.pallas_call(rows_kernel, out_shape=jax.ShapeDtypeStruct((rows, cols),...  5.76 us
    dot_general x1, matrix products, per_device(): jnp.dot(err_scaled, head_weight.T, preferred_element_type=jnp.float32)  5.48 us
  transfers between devices with their start and end apart: 3, of which 2 were waited for; matrix products, arithmetic and copies ran while one was open for 6% of the time, Pallas kernels for 2%

profile of v3, /device:TPU:0, one launch (start us, length us, event | category | flops | bytes accessed | tf_op | source)
XLA Modules:
  0.0 257.4 jit_solution(6600915900866086400)
XLA Ops:
  0.6 0.0 copy-start
  0.6 0.8 broadcast_add_fusion
  1.5 0.9 select_reduce_fusion
  2.4 0.1 copy.15
  2.5 15.4 %all_to_all.14 = s32[16,1,1]{2,1,0:T(1,128)S(1)} all-to-all(s32[16,1,1]{2,1,0:T(1,128)S(1)} %copy.15), channel_id=1, replica_groups=mesh['dp'=16,'mp'=2] {'dp'}, dimensions={0} | all-to-all | bytes 128 | tf_op jit(solution)/shard_map/all_to_all | solution.py:320
  17.9 0.4 maximum_reduce_fusion
  18.3 0.0 copy-done
  18.3 2.7 %gather_fusion = bf16[16,64,1600]{2,1,0:T(8,128)(2,1)} fusion(bf16[16,64,1600]{2,1,0:T(8,128)(2,1)S(1)} %copy-done, s32[1024]{0:T(1024)S(1)} %pad_clamp_fusion), kind=kCustom, calls=%fused_computation | custom fusion | bytes 6553664 | tf_op jit(solution)/shard_map/jit(_take)/gather | solution.py:331
  21.0 4.5 %all-to-all-start.1 = ((bf16[16,64,1600]{2,1,0:T(8,128)(2,1)}), bf16[16,64,1600]{2,1,0:T(8,128)(2,1)}, u32[]{:S(2)}, u32[]{:S(2)}) async-start(bf16[16,64,1600]{2,1,0:T(8,128)(2,1)} %gather_fusion), calls=%async_computation.1 | async-start | bytes 6815744 | tf_op jit(solution)/shard_map/all_to_all | solution.py:332
  25.5 1.4 convert_reduce_fusion
  26.9 1.6 fusion.11
  28.6 0.0 copy-start.9
  28.6 5.1 %fusion.16 = f32[512,2048]{1,0:T(8,128)S(1)} fusion(bf16[1024,2048]{1,0:T(8,128)(2,1)} %param.11, bf16[512,1024]{1,0:T(8,128)(2,1)} %param.7, f32[512]{0:T(512)S(1)} %add_rsqrt_fusion.1, f32[512]{0:T(512)S(1)} %broadcast_multiply_fusion.3), kind=kOutput, calls=%fused_computation.42 | convolution fusion | flops 2149580800 | bytes 9441280 | tf_op jit(solution)/shard_map/dot_general | solution.py:324
  33.7 0.0 copy-done.9
  33.7 0.0 copy-start.11
  33.7 0.0 copy-start.2
  33.7 2.7 %convolution_convert_fusion.3 = bf16[512,1024]{1,0:T(8,128)(2,1)S(1)} fusion(bf16[2048,1024]{1,0:T(8,128)(2,1)S(1)} %copy-done.9, f32[512,2048]{1,0:T(8,128)S(1)} %fusion.16), kind=kOutput, calls=%fused_computation.30 | convolution fusion | flops 2157445120 | bytes 9437184 | tf_op jit(solution)/shard_map/dot_general | solution.py:326
  36.4 0.0 copy-done.11
  36.4 0.0 copy-start.4
  36.4 0.1 collective-permute-start
  36.5 2.6 %collective-permute-done = bf16[512,1024]{1,0:T(8,128)(2,1)S(1)} collective-permute-done((bf16[512,1024]{1,0:T(8,128)(2,1)S(1)}, bf16[512,1024]{1,0:T(8,128)(2,1)S(1)}, u32[]{:S(2)}, u32[]{:S(2)}) %collective-permute-start) | collective-permute-done | bytes 1048608 | tf_op jit(solution)/shard_map/ppermute | solution.py:37
  39.2 0.0 copy-done.2
  39.2 0.5 fusion.18
  39.7 0.0 copy-start.10
  39.7 0.7 multiply_reduce_fusion.1
  40.4 0.0 copy-done.6
  40.4 0.6 fusion.14.left_ref
  41.0 0.0 copy-done.4
  41.0 0.0 copy-start.8
  41.0 1.0 copy-done.8
  42.0 0.0 copy-done.10
  42.0 3.8 %fusion.19.pred_ref = f32[512,1600]{1,0:T(8,128)} fusion(bf16[512,1024]{1,0:T(8,128)(2,1)S(1)} %fusion.14.left_ref, bf16[1024,1600]{0,1:T(8,128)(2,1)S(1)} %copy-done.10), kind=kOutput, calls=%fused_computation.44 | convolution fusion | flops 1677721600 | bytes 7602176 | tf_op jit(solution)/shard_map/dot_general | solution.py:333
  45.8 44.6 %all-to-all-done.1.block_ref = bf16[16,64,1600]{2,1,0:T(8,128)(2,1)} async-done(((bf16[16,64,1600]{2,1,0:T(8,128)(2,1)}), bf16[16,64,1600]{2,1,0:T(8,128)(2,1)}, u32[]{:S(2)}, u32[]{:S(2)}) %all-to-all-start.1) | async-done | bytes 3276832 | tf_op jit(solution)/shard_map/all_to_all | solution.py:332
  90.4 6.9 %shard_map.94.right_ref = bf16[512,1600]{1,0:T(8,128)(2,1)} custom-call(s32[8]{0:T(128)} %owner_ref.1, f32[512,1600]{1,0:T(8,128)} %fusion.19.pred_ref, bf16[16,64,1600]{2,1,0:T(8,128)(2,1)} %all-to-all-done.1.block_ref), custom_call_target="tpu_custom_call" | custom-call | flops 1638400 | bytes 6553600 | tf_op jit(solution)/shard_map/pallas_call | solution.py:264
  97.3 5.5 %convolution_convert_fusion.2 = bf16[512,1024]{1,0:T(8,128)(2,1)} fusion(bf16[512,1600]{1,0:T(8,128)(2,1)} %shard_map.94.right_ref, bf16[1024,1600]{0,1:T(8,128)(2,1)} %param.13), kind=kOutput, calls=%fused_computation.29 | convolution fusion | flops 1678245888 | bytes 5963776 | tf_op jit(solution)/shard_map/dot_general | solution.py:336
  102.8 0.0 collective-permute-start.1
  102.8 5.8 %shard_map.95 = bf16[1024,1600]{1,0:T(8,128)(2,1)} custom-call(bf16[512,1024]{1,0:T(8,128)(2,1)} %copy-done.8, bf16[512,1600]{1,0:T(8,128)(2,1)} %shard_map.94.right_ref), custom_call_target="tpu_custom_call" | custom-call | flops 1677721600 | bytes 5963776 | tf_op jit(solution)/shard_map/pallas_call | solution.py:292
  108.5 0.0 collective-permute-done.1
  108.6 3.7 %fusion.13 = (f32[512]{0:T(512)S(1)}, f32[512]{0:T(512)S(1)}) fusion(bf16[512,1024]{1,0:T(8,128)(2,1)} %collective-permute-done.1, bf16[512,1024]{1,0:T(8,128)(2,1)} %convolution_convert_fusion.2, f32[512]{0:T(512)S(1)} %add_rsqrt_fusion, f32[512]{0:T(512)S(1)} %broadcast_multiply_fusion.2, bf16[512,1024]{1,0:T(8,128)(2,1)} %copy-done.6, ...), kind=kLoop, calls=%fused_computation.27 | loop fusion | flops 6814720 | bytes 5251072 | tf_op jit(solution)/shard_map/reduce_sum | solution.py:340
  112.2 0.0 copy-done.3
  112.2 0.0 copy-done.5
  112.2 3.5 %multiply_convert_fusion.1 = bf16[512,1024]{1,0:T(8,128)(2,1)} fusion(bf16[512,1024]{1,0:T(8,128)(2,1)} %collective-permute-done.1, bf16[512,1024]{1,0:T(8,128)(2,1)} %convolution_convert_fusion.2, f32[512]{0:T(512)S(1)} %get-tuple-element.11, f32[512]{0:T(512)S(1)} %get-tuple-element.12, f32[512]{0:T(512)S(1)} %add_rsqrt_fusion, ...), kind=kLoop, calls=%fused_computation.22 | loop fusion | flops 7864320 | bytes 6299648 | tf_op jit(solution)/shard_map/convert_element_type | solution.py:343
  115.8 10.7 %convolution_convert_fusion = bf16[1024,2048]{1,0:T(8,128)(2,1)} fusion(bf16[512,1024]{1,0:T(8,128)(2,1)} %param.7, f32[512]{0:T(512)S(1)} %add_rsqrt_fusion.1, f32[512]{0:T(512)S(1)} %broadcast_multiply_fusion.3, f32[512,2048]{1,0:T(8,128)} %copy-done.11, bf16[512,1024]{1,0:T(8,128)(2,1)} %multiply_convert_fusion.1, bf16[2048,1024]{1,0:T(8,128)(2,1)} %param.12), kind=kOutput, calls=%fused_computation.13 | convolution fusion | flops 4319084544 | bytes 14684160 | tf_op jit(solution)/shard_map/dot_general | solution.py:347
  126.4 7.2 %convolution_convert_fusion.1 = bf16[1024,2048]{1,0:T(8,128)(2,1)} fusion(bf16[512,1024]{1,0:T(8,128)(2,1)} %multiply_convert_fusion.1, f32[512,2048]{1,0:T(8,128)} %copy-done.11), kind=kOutput, calls=%fused_computation.14 | convolution fusion | flops 2159017984 | bytes 9437184 | tf_op jit(solution)/shard_map/dot_general | solution.py:344
  133.7 121.4 %shard_map.96 = (f32[64,1600]{1,0:T(8,128)S(1)}, f32[64,2048]{1,0:T(8,128)S(1)}, f32[64,2048]{1,0:T(8,128)S(1)}) custom-call(bf16[4,2,2,64,1600]{4,3,2,1,0:T(8,128)(2,1)S(1)} %bitcast.23, bf16[4,2,2,64,2048]{4,3,2,1,0:T(8,128)(2,1)} %bitcast.26, bf16[4,2,2,64,2048]{4,3,2,1,0:T(8,128)(2,1)} %bitcast.25), custom_call_target="tpu_custom_call" | custom-call | tf_op jit(solution)/shard_map/pallas_call | solution.py:238
  255.1 0.8 copy.21
  255.9 0.8 copy.22
  256.7 0.8 copy.23
  (13 shorter events, 0.1 us)
Async XLA Ops:
  0.6 17.7 %copy-start = (bf16[16,64,1600]{2,1,0:T(8,128)(2,1)S(1)}, bf16[16,64,1600]{2,1,0:T(8,128)(2,1)}, u32[]{:S(2)}) copy-start(bf16[16,64,1600]{2,1,0:T(8,128)(2,1)} %param.10) | copy-start | bytes 9830404
  21.0 69.4 %all-to-all-start.1 = ((bf16[16,64,1600]{2,1,0:T(8,128)(2,1)}), bf16[16,64,1600]{2,1,0:T(8,128)(2,1)}, u32[]{:S(2)}, u32[]{:S(2)}) async-start(bf16[16,64,1600]{2,1,0:T(8,128)(2,1)} %gather_fusion), calls=%async_computation.1 | async-start | bytes 6815744 | tf_op jit(solution)/shard_map/all_to_all | solution.py:332
  28.6 5.1 %copy-start.9 = (bf16[2048,1024]{1,0:T(8,128)(2,1)S(1)}, bf16[2048,1024]{1,0:T(8,128)(2,1)}, u32[]{:S(2)}) copy-start(bf16[2048,1024]{1,0:T(8,128)(2,1)} %param.12) | copy-start | bytes 12582916
  33.7 2.7 %copy-start.11 = (f32[512,2048]{1,0:T(8,128)}, f32[512,2048]{1,0:T(8,128)S(1)}, u32[]{:S(2)}) copy-start(f32[512,2048]{1,0:T(8,128)S(1)} %fusion.16) | copy-start | bytes 12582916
  33.7 5.4 %copy-start.2 = (bf16[512,1024]{1,0:T(8,128)(2,1)S(1)}, bf16[512,1024]{1,0:T(8,128)(2,1)}, u32[]{:S(2)}) copy-start(bf16[512,1024]{1,0:T(8,128)(2,1)} %param.7) | copy-start | bytes 3145732
  36.4 4.5 %copy-start.4 = (bf16[512,1024]{1,0:T(8,128)(2,1)}, bf16[512,1024]{1,0:T(8,128)(2,1)S(1)}, u32[]{:S(2)}) copy-start(bf16[512,1024]{1,0:T(8,128)(2,1)S(1)} %convolution_convert_fusion.3) | copy-start | bytes 3145732
  36.4 2.7 %collective-permute-start = (bf16[512,1024]{1,0:T(8,128)(2,1)S(1)}, bf16[512,1024]{1,0:T(8,128)(2,1)S(1)}, u32[]{:S(2)}, u32[]{:S(2)}) collective-permute-start(bf16[512,1024]{1,0:T(8,128)(2,1)S(1)} %convolution_convert_fusion.3), channel_id=1, source_target_pairs={{0,1},{1,0},{2,3},{3,2},{4,5},{5,4},{6,7},{7,6},{8,9},{9,8},{10,11... | collective-permute-start | bytes 3145736 | tf_op jit(solution)/shard_map/ppermute | solution.py:37
  39.2 1.2 copy-start.6
  39.7 2.3 copy-start.10
  41.0 1.0 copy-start.8
  102.8 5.8 %collective-permute-start.1 = (bf16[512,1024]{1,0:T(8,128)(2,1)}, bf16[512,1024]{1,0:T(8,128)(2,1)}, u32[]{:S(2)}, u32[]{:S(2)}) collective-permute-start(bf16[512,1024]{1,0:T(8,128)(2,1)} %convolution_convert_fusion.2), channel_id=1, source_target_pairs={{0,1},{1,0},{2,3},{3,2},{4,5},{5,4},{6,7},{7,6},{8,9},{9,8},{10,11... | collective-permute-start | bytes 3145736 | tf_op jit(solution)/shard_map/ppermute | solution.py:37
  108.5 3.7 %copy-start.3 = (bf16[512,1024]{1,0:T(8,128)(2,1)S(1)}, bf16[512,1024]{1,0:T(8,128)(2,1)}, u32[]{:S(2)}) copy-start(bf16[512,1024]{1,0:T(8,128)(2,1)} %param.7) | copy-start | bytes 3145732
  108.5 3.7 %copy-start.5 = (bf16[512,1024]{1,0:T(8,128)(2,1)S(1)}, bf16[512,1024]{1,0:T(8,128)(2,1)}, u32[]{:S(2)}) copy-start(bf16[512,1024]{1,0:T(8,128)(2,1)} %copy-done.4) | copy-start | bytes 3145732
  108.5 3.7 %copy-start.7 = (bf16[512,1024]{1,0:T(8,128)(2,1)S(1)}, bf16[512,1024]{1,0:T(8,128)(2,1)}, u32[]{:S(2)}) copy-start(bf16[512,1024]{1,0:T(8,128)(2,1)} %copy-done.6) | copy-start | bytes 3145732
  126.4 7.2 %copy-start.1 = (bf16[1024,1600]{1,0:T(8,128)(2,1)S(1)}, bf16[1024,1600]{1,0:T(8,128)(2,1)}, u32[]{:S(2)}) copy-start(bf16[1024,1600]{1,0:T(8,128)(2,1)} %shard_map.95) | copy-start | bytes 9830404

commit v4 on v3

--- a/solution.py
+++ b/solution.py
@@ -207,8 +207,9 @@
             lax.fori_loop(0, blocks, add, 0)
 
     groups = plan.groups
-    ahead = 2
-    for group in [groups[0], plan.early, *groups[1:ahead]]:
+    ahead = 3
+    first = [[c for c in group if c not in plan.early] for group in groups]
+    for group in [first[0], plan.early, *first[1:ahead]]:
         for chunk in group:
             launch(chunk, 0)
     for step in range(len(groups) + stages - 1):
@@ -219,9 +220,8 @@
                     if stage + 1 < stages:
                         launch(chunk, stage + 1)
                 if stage == 0 and step + ahead < len(groups):
-                    for chunk in groups[step + ahead]:
-                        if chunk not in plan.early:
-                            launch(chunk, 0)
+                    for chunk in first[step + ahead]:
+                        launch(chunk, 0)
     for chunk in range(len(plan.chunks)):
         for stage in range(stages):
             for copy in sends(chunk, stage):

time: 258 us -> 263 us (1.019)
  Pallas kernels: 134 us -> 139 us
    pallas_call x1, Pallas kernels: 121 us -> 127 us  [scatter_sum(): pl.pallas_call(functools.partial(scatter_kernel, plan, len(grads)), out_s...]
where the time goes in v4:
time: 263 us
  Pallas kernels  139 us (53%)
  waiting for transfers between devices  47.2 us (18%)
  matrix products  35 us (13%)
  blocking collectives  15.4 us (6%)
  other arithmetic  14.2 us (5%)
  local copies, waits for them, and re-layouts  6.16 us (2%)
  starting transfers between devices  4.57 us (2%)
    pallas_call x1, Pallas kernels, scatter_sum(): pl.pallas_call(functools.partial(scatter_kernel, plan, len(grads)), out_s...  127 us
    all_to_all x1, waiting for transfers between devices, per_device(): lax.all_to_all(stored, 'dp', split_axis=0, concat_axis=0, tiled=True)  44.6 us
    all_to_all x1, blocking collectives, per_device(): lax.all_to_all(request, 'dp', split_axis=0, concat_axis=0, tiled=True)  15.4 us
    dot_general x1, matrix products, per_device(): fc_grad = jnp.dot(normed_in.T, grad_pre, preferred_element_type=jnp.float32)  10.7 us
    dot_general x1, matrix products, per_device(): jnp.dot(grad_hidden.T, act_out, preferred_element_type=jnp.float32)  7.22 us
    pallas_call x1, Pallas kernels, scaled_error(): pl.pallas_call(functools.partial(error_kernel, scale), out_shape=jax.Shap...  6.89 us
    pallas_call x1, Pallas kernels, outer_product(): pl.pallas_call(rows_kernel, out_shape=jax.ShapeDtypeStruct((rows, cols),...  5.76 us
    dot_general x1, matrix products, per_device(): jnp.dot(err_scaled, head_weight.T, preferred_element_type=jnp.float32)  5.48 us
  transfers between devices with their start and end apart: 3, of which 2 were waited for; matrix products, arithmetic and copies ran while one was open for 6% of the time, Pallas kernels for 2%

profile of v4, /device:TPU:0, one launch (start us, length us, event | category | flops | bytes accessed | tf_op | source)
XLA Modules:
  0.0 262.8 jit_solution(4200609602799470885)
XLA Ops:
  0.6 0.0 copy-start
  0.6 0.8 broadcast_add_fusion
  1.5 0.9 select_reduce_fusion
  2.4 0.1 copy.15
  2.5 15.4 %all_to_all.14 = s32[16,1,1]{2,1,0:T(1,128)S(1)} all-to-all(s32[16,1,1]{2,1,0:T(1,128)S(1)} %copy.15), channel_id=1, replica_groups=mesh['dp'=16,'mp'=2] {'dp'}, dimensions={0} | all-to-all | bytes 128 | tf_op jit(solution)/shard_map/all_to_all | solution.py:320
  17.9 0.4 maximum_reduce_fusion
  18.3 0.0 copy-done
  18.3 2.7 %gather_fusion = bf16[16,64,1600]{2,1,0:T(8,128)(2,1)} fusion(bf16[16,64,1600]{2,1,0:T(8,128)(2,1)S(1)} %copy-done, s32[1024]{0:T(1024)S(1)} %pad_clamp_fusion), kind=kCustom, calls=%fused_computation | custom fusion | bytes 6553664 | tf_op jit(solution)/shard_map/jit(_take)/gather | solution.py:331
  21.0 4.5 %all-to-all-start.1 = ((bf16[16,64,1600]{2,1,0:T(8,128)(2,1)}), bf16[16,64,1600]{2,1,0:T(8,128)(2,1)}, u32[]{:S(2)}, u32[]{:S(2)}) async-start(bf16[16,64,1600]{2,1,0:T(8,128)(2,1)} %gather_fusion), calls=%async_computation.1 | async-start | bytes 6815744 | tf_op jit(solution)/shard_map/all_to_all | solution.py:332
  25.5 1.4 convert_reduce_fusion
  26.9 1.6 fusion.11
  28.6 0.0 copy-start.9
  28.6 5.1 %fusion.16 = f32[512,2048]{1,0:T(8,128)S(1)} fusion(bf16[1024,2048]{1,0:T(8,128)(2,1)} %param.11, bf16[512,1024]{1,0:T(8,128)(2,1)} %param.7, f32[512]{0:T(512)S(1)} %add_rsqrt_fusion.1, f32[512]{0:T(512)S(1)} %broadcast_multiply_fusion.3), kind=kOutput, calls=%fused_computation.42 | convolution fusion | flops 2149580800 | bytes 9441280 | tf_op jit(solution)/shard_map/dot_general | solution.py:324
  33.7 0.0 copy-done.9
  33.7 0.0 copy-start.11
  33.7 0.0 copy-start.2
  33.7 2.7 %convolution_convert_fusion.3 = bf16[512,1024]{1,0:T(8,128)(2,1)S(1)} fusion(bf16[2048,1024]{1,0:T(8,128)(2,1)S(1)} %copy-done.9, f32[512,2048]{1,0:T(8,128)S(1)} %fusion.16), kind=kOutput, calls=%fused_computation.30 | convolution fusion | flops 2157445120 | bytes 9437184 | tf_op jit(solution)/shard_map/dot_general | solution.py:326
  36.4 0.0 copy-done.11
  36.4 0.0 copy-start.4
  36.4 0.1 collective-permute-start
  36.5 2.6 %collective-permute-done = bf16[512,1024]{1,0:T(8,128)(2,1)S(1)} collective-permute-done((bf16[512,1024]{1,0:T(8,128)(2,1)S(1)}, bf16[512,1024]{1,0:T(8,128)(2,1)S(1)}, u32[]{:S(2)}, u32[]{:S(2)}) %collective-permute-start) | collective-permute-done | bytes 1048608 | tf_op jit(solution)/shard_map/ppermute | solution.py:37
  39.2 0.0 copy-done.2
  39.2 0.5 fusion.18
  39.7 0.0 copy-start.10
  39.7 0.7 multiply_reduce_fusion.1
  40.4 0.0 copy-done.6
  40.4 0.6 fusion.14.left_ref
  41.0 0.0 copy-done.4
  41.0 0.0 copy-start.8
  41.0 1.0 copy-done.8
  42.0 0.0 copy-done.10
  42.0 3.8 %fusion.19.pred_ref = f32[512,1600]{1,0:T(8,128)} fusion(bf16[512,1024]{1,0:T(8,128)(2,1)S(1)} %fusion.14.left_ref, bf16[1024,1600]{0,1:T(8,128)(2,1)S(1)} %copy-done.10), kind=kOutput, calls=%fused_computation.44 | convolution fusion | flops 1677721600 | bytes 7602176 | tf_op jit(solution)/shard_map/dot_general | solution.py:333
  45.8 44.6 %all-to-all-done.1.block_ref = bf16[16,64,1600]{2,1,0:T(8,128)(2,1)} async-done(((bf16[16,64,1600]{2,1,0:T(8,128)(2,1)}), bf16[16,64,1600]{2,1,0:T(8,128)(2,1)}, u32[]{:S(2)}, u32[]{:S(2)}) %all-to-all-start.1) | async-done | bytes 3276832 | tf_op jit(solution)/shard_map/all_to_all | solution.py:332
  90.4 6.9 %shard_map.94.right_ref = bf16[512,1600]{1,0:T(8,128)(2,1)} custom-call(s32[8]{0:T(128)} %owner_ref.1, f32[512,1600]{1,0:T(8,128)} %fusion.19.pred_ref, bf16[16,64,1600]{2,1,0:T(8,128)(2,1)} %all-to-all-done.1.block_ref), custom_call_target="tpu_custom_call" | custom-call | flops 1638400 | bytes 6553600 | tf_op jit(solution)/shard_map/pallas_call | solution.py:264
  97.3 5.5 %convolution_convert_fusion.2 = bf16[512,1024]{1,0:T(8,128)(2,1)} fusion(bf16[512,1600]{1,0:T(8,128)(2,1)} %shard_map.94.right_ref, bf16[1024,1600]{0,1:T(8,128)(2,1)} %param.13), kind=kOutput, calls=%fused_computation.29 | convolution fusion | flops 1678245888 | bytes 5963776 | tf_op jit(solution)/shard_map/dot_general | solution.py:336
  102.8 0.0 collective-permute-start.1
  102.8 5.8 %shard_map.95 = bf16[1024,1600]{1,0:T(8,128)(2,1)} custom-call(bf16[512,1024]{1,0:T(8,128)(2,1)} %copy-done.8, bf16[512,1600]{1,0:T(8,128)(2,1)} %shard_map.94.right_ref), custom_call_target="tpu_custom_call" | custom-call | flops 1677721600 | bytes 5963776 | tf_op jit(solution)/shard_map/pallas_call | solution.py:292
  108.5 0.0 collective-permute-done.1
  108.6 3.7 %fusion.13 = (f32[512]{0:T(512)S(1)}, f32[512]{0:T(512)S(1)}) fusion(bf16[512,1024]{1,0:T(8,128)(2,1)} %collective-permute-done.1, bf16[512,1024]{1,0:T(8,128)(2,1)} %convolution_convert_fusion.2, f32[512]{0:T(512)S(1)} %add_rsqrt_fusion, f32[512]{0:T(512)S(1)} %broadcast_multiply_fusion.2, bf16[512,1024]{1,0:T(8,128)(2,1)} %copy-done.6, ...), kind=kLoop, calls=%fused_computation.27 | loop fusion | flops 6814720 | bytes 5251072 | tf_op jit(solution)/shard_map/reduce_sum | solution.py:340
  112.2 0.0 copy-done.3
  112.2 0.0 copy-done.5
  112.2 3.5 %multiply_convert_fusion.1 = bf16[512,1024]{1,0:T(8,128)(2,1)} fusion(bf16[512,1024]{1,0:T(8,128)(2,1)} %collective-permute-done.1, bf16[512,1024]{1,0:T(8,128)(2,1)} %convolution_convert_fusion.2, f32[512]{0:T(512)S(1)} %get-tuple-element.11, f32[512]{0:T(512)S(1)} %get-tuple-element.12, f32[512]{0:T(512)S(1)} %add_rsqrt_fusion, ...), kind=kLoop, calls=%fused_computation.22 | loop fusion | flops 7864320 | bytes 6299648 | tf_op jit(solution)/shard_map/convert_element_type | solution.py:343
  115.8 10.7 %convolution_convert_fusion = bf16[1024,2048]{1,0:T(8,128)(2,1)} fusion(bf16[512,1024]{1,0:T(8,128)(2,1)} %param.7, f32[512]{0:T(512)S(1)} %add_rsqrt_fusion.1, f32[512]{0:T(512)S(1)} %broadcast_multiply_fusion.3, f32[512,2048]{1,0:T(8,128)} %copy-done.11, bf16[512,1024]{1,0:T(8,128)(2,1)} %multiply_convert_fusion.1, bf16[2048,1024]{1,0:T(8,128)(2,1)} %param.12), kind=kOutput, calls=%fused_computation.13 | convolution fusion | flops 4319084544 | bytes 14684160 | tf_op jit(solution)/shard_map/dot_general | solution.py:347
  126.4 7.2 %convolution_convert_fusion.1 = bf16[1024,2048]{1,0:T(8,128)(2,1)} fusion(bf16[512,1024]{1,0:T(8,128)(2,1)} %multiply_convert_fusion.1, f32[512,2048]{1,0:T(8,128)} %copy-done.11), kind=kOutput, calls=%fused_computation.14 | convolution fusion | flops 2159017984 | bytes 9437184 | tf_op jit(solution)/shard_map/dot_general | solution.py:344
  133.7 126.8 %shard_map.96 = (f32[64,1600]{1,0:T(8,128)S(1)}, f32[64,2048]{1,0:T(8,128)S(1)}, f32[64,2048]{1,0:T(8,128)S(1)}) custom-call(bf16[4,2,2,64,1600]{4,3,2,1,0:T(8,128)(2,1)S(1)} %bitcast.23, bf16[4,2,2,64,2048]{4,3,2,1,0:T(8,128)(2,1)} %bitcast.26, bf16[4,2,2,64,2048]{4,3,2,1,0:T(8,128)(2,1)} %bitcast.25), custom_call_target="tpu_custom_call" | custom-call | tf_op jit(solution)/shard_map/pallas_call | solution.py:238
  260.5 0.8 copy.21
  261.2 0.8 copy.22
  262.0 0.8 copy.23
  (13 shorter events, 0.1 us)
Async XLA Ops:
  0.6 17.7 %copy-start = (bf16[16,64,1600]{2,1,0:T(8,128)(2,1)S(1)}, bf16[16,64,1600]{2,1,0:T(8,128)(2,1)}, u32[]{:S(2)}) copy-start(bf16[16,64,1600]{2,1,0:T(8,128)(2,1)} %param.10) | copy-start | bytes 9830404
  21.0 69.4 %all-to-all-start.1 = ((bf16[16,64,1600]{2,1,0:T(8,128)(2,1)}), bf16[16,64,1600]{2,1,0:T(8,128)(2,1)}, u32[]{:S(2)}, u32[]{:S(2)}) async-start(bf16[16,64,1600]{2,1,0:T(8,128)(2,1)} %gather_fusion), calls=%async_computation.1 | async-start | bytes 6815744 | tf_op jit(solution)/shard_map/all_to_all | solution.py:332
  28.6 5.1 %copy-start.9 = (bf16[2048,1024]{1,0:T(8,128)(2,1)S(1)}, bf16[2048,1024]{1,0:T(8,128)(2,1)}, u32[]{:S(2)}) copy-start(bf16[2048,1024]{1,0:T(8,128)(2,1)} %param.12) | copy-start | bytes 12582916
  33.7 2.7 %copy-start.11 = (f32[512,2048]{1,0:T(8,128)}, f32[512,2048]{1,0:T(8,128)S(1)}, u32[]{:S(2)}) copy-start(f32[512,2048]{1,0:T(8,128)S(1)} %fusion.16) | copy-start | bytes 12582916
  33.7 5.4 %copy-start.2 = (bf16[512,1024]{1,0:T(8,128)(2,1)S(1)}, bf16[512,1024]{1,0:T(8,128)(2,1)}, u32[]{:S(2)}) copy-start(bf16[512,1024]{1,0:T(8,128)(2,1)} %param.7) | copy-start | bytes 3145732
  36.4 4.5 %copy-start.4 = (bf16[512,1024]{1,0:T(8,128)(2,1)}, bf16[512,1024]{1,0:T(8,128)(2,1)S(1)}, u32[]{:S(2)}) copy-start(bf16[512,1024]{1,0:T(8,128)(2,1)S(1)} %convolution_convert_fusion.3) | copy-start | bytes 3145732
  36.4 2.7 %collective-permute-start = (bf16[512,1024]{1,0:T(8,128)(2,1)S(1)}, bf16[512,1024]{1,0:T(8,128)(2,1)S(1)}, u32[]{:S(2)}, u32[]{:S(2)}) collective-permute-start(bf16[512,1024]{1,0:T(8,128)(2,1)S(1)} %convolution_convert_fusion.3), channel_id=1, source_target_pairs={{0,1},{1,0},{2,3},{3,2},{4,5},{5,4},{6,7},{7,6},{8,9},{9,8},{10,11... | collective-permute-start | bytes 3145736 | tf_op jit(solution)/shard_map/ppermute | solution.py:37
  39.2 1.2 copy-start.6
  39.7 2.3 copy-start.10
  41.0 1.0 copy-start.8
  102.8 5.8 %collective-permute-start.1 = (bf16[512,1024]{1,0:T(8,128)(2,1)}, bf16[512,1024]{1,0:T(8,128)(2,1)}, u32[]{:S(2)}, u32[]{:S(2)}) collective-permute-start(bf16[512,1024]{1,0:T(8,128)(2,1)} %convolution_convert_fusion.2), channel_id=1, source_target_pairs={{0,1},{1,0},{2,3},{3,2},{4,5},{5,4},{6,7},{7,6},{8,9},{9,8},{10,11... | collective-permute-start | bytes 3145736 | tf_op jit(solution)/shard_map/ppermute | solution.py:37
  108.5 3.7 %copy-start.3 = (bf16[512,1024]{1,0:T(8,128)(2,1)S(1)}, bf16[512,1024]{1,0:T(8,128)(2,1)}, u32[]{:S(2)}) copy-start(bf16[512,1024]{1,0:T(8,128)(2,1)} %param.7) | copy-start | bytes 3145732
  108.5 3.7 %copy-start.5 = (bf16[512,1024]{1,0:T(8,128)(2,1)S(1)}, bf16[512,1024]{1,0:T(8,128)(2,1)}, u32[]{:S(2)}) copy-start(bf16[512,1024]{1,0:T(8,128)(2,1)} %copy-done.4) | copy-start | bytes 3145732
  108.5 3.7 %copy-start.7 = (bf16[512,1024]{1,0:T(8,128)(2,1)S(1)}, bf16[512,1024]{1,0:T(8,128)(2,1)}, u32[]{:S(2)}) copy-start(bf16[512,1024]{1,0:T(8,128)(2,1)} %copy-done.6) | copy-start | bytes 3145732
  126.4 7.2 %copy-start.1 = (bf16[1024,1600]{1,0:T(8,128)(2,1)S(1)}, bf16[1024,1600]{1,0:T(8,128)(2,1)}, u32[]{:S(2)}) copy-start(bf16[1024,1600]{1,0:T(8,128)(2,1)} %shard_map.95) | copy-start | bytes 9830404

commit v5 on v3

--- a/solution.py
+++ b/solution.py
@@ -218,10 +218,10 @@
                     finish(chunk, stage)
                     if stage + 1 < stages:
                         launch(chunk, stage + 1)
-                if stage == 0 and step + ahead < len(groups):
-                    for chunk in groups[step + ahead]:
-                        if chunk not in plan.early:
-                            launch(chunk, 0)
+        if step + ahead < len(groups):
+            for chunk in groups[step + ahead]:
+                if chunk not in plan.early:
+                    launch(chunk, 0)
     for chunk in range(len(plan.chunks)):
         for stage in range(stages):
             for copy in sends(chunk, stage):

time: 258 us -> 258 us (level)
  no operation moved by 1% of the time
where the time goes in v5:
time: 258 us; the launch traced here: 257 us
  Pallas kernels  134 us (52%)
  waiting for transfers between devices  47.2 us (18%)
  matrix products  35 us (14%)
  blocking collectives  15.4 us (6%)
  other arithmetic  14.2 us (6%)
  local copies, waits for them, and re-layouts  6.16 us (2%)
  starting transfers between devices  4.57 us (2%)
    pallas_call x1, Pallas kernels, scatter_sum(): pl.pallas_call(functools.partial(scatter_kernel, plan, len(grads)), out_s...  121 us
    all_to_all x1, waiting for transfers between devices, per_device(): lax.all_to_all(stored, 'dp', split_axis=0, concat_axis=0, tiled=True)  44.6 us
    all_to_all x1, blocking collectives, per_device(): lax.all_to_all(request, 'dp', split_axis=0, concat_axis=0, tiled=True)  15.4 us
    dot_general x1, matrix products, per_device(): fc_grad = jnp.dot(normed_in.T, grad_pre, preferred_element_type=jnp.float32)  10.7 us
    dot_general x1, matrix products, per_device(): jnp.dot(grad_hidden.T, act_out, preferred_element_type=jnp.float32)  7.22 us
    pallas_call x1, Pallas kernels, scaled_error(): pl.pallas_call(functools.partial(error_kernel, scale), out_shape=jax.Shap...  6.89 us
    pallas_call x1, Pallas kernels, outer_product(): pl.pallas_call(rows_kernel, out_shape=jax.ShapeDtypeStruct((rows, cols),...  5.76 us
    dot_general x1, matrix products, per_device(): jnp.dot(err_scaled, head_weight.T, preferred_element_type=jnp.float32)  5.48 us
  transfers between devices with their start and end apart: 3, of which 2 were waited for; matrix products, arithmetic and copies ran while one was open for 6% of the time, Pallas kernels for 2%

profile of v5, /device:TPU:0, one launch (start us, length us, event | category | flops | bytes accessed | tf_op | source)
XLA Modules:
  0.0 257.4 jit_solution(7361825077764925759)
XLA Ops:
  0.6 0.0 copy-start
  0.6 0.8 broadcast_add_fusion
  1.5 0.9 select_reduce_fusion
  2.4 0.1 copy.15
  2.5 15.4 %all_to_all.14 = s32[16,1,1]{2,1,0:T(1,128)S(1)} all-to-all(s32[16,1,1]{2,1,0:T(1,128)S(1)} %copy.15), channel_id=1, replica_groups=mesh['dp'=16,'mp'=2] {'dp'}, dimensions={0} | all-to-all | bytes 128 | tf_op jit(solution)/shard_map/all_to_all | solution.py:320
  17.9 0.4 maximum_reduce_fusion
  18.3 0.0 copy-done
  18.3 2.7 %gather_fusion = bf16[16,64,1600]{2,1,0:T(8,128)(2,1)} fusion(bf16[16,64,1600]{2,1,0:T(8,128)(2,1)S(1)} %copy-done, s32[1024]{0:T(1024)S(1)} %pad_clamp_fusion), kind=kCustom, calls=%fused_computation | custom fusion | bytes 6553664 | tf_op jit(solution)/shard_map/jit(_take)/gather | solution.py:331
  21.0 4.5 %all-to-all-start.1 = ((bf16[16,64,1600]{2,1,0:T(8,128)(2,1)}), bf16[16,64,1600]{2,1,0:T(8,128)(2,1)}, u32[]{:S(2)}, u32[]{:S(2)}) async-start(bf16[16,64,1600]{2,1,0:T(8,128)(2,1)} %gather_fusion), calls=%async_computation.1 | async-start | bytes 6815744 | tf_op jit(solution)/shard_map/all_to_all | solution.py:332
  25.5 1.4 convert_reduce_fusion
  26.9 1.6 fusion.11
  28.6 0.0 copy-start.9
  28.6 5.1 %fusion.16 = f32[512,2048]{1,0:T(8,128)S(1)} fusion(bf16[1024,2048]{1,0:T(8,128)(2,1)} %param.11, bf16[512,1024]{1,0:T(8,128)(2,1)} %param.7, f32[512]{0:T(512)S(1)} %add_rsqrt_fusion.1, f32[512]{0:T(512)S(1)} %broadcast_multiply_fusion.3), kind=kOutput, calls=%fused_computation.42 | convolution fusion | flops 2149580800 | bytes 9441280 | tf_op jit(solution)/shard_map/dot_general | solution.py:324
  33.7 0.0 copy-done.9
  33.7 0.0 copy-start.11
  33.7 0.0 copy-start.2
  33.7 2.7 %convolution_convert_fusion.3 = bf16[512,1024]{1,0:T(8,128)(2,1)S(1)} fusion(bf16[2048,1024]{1,0:T(8,128)(2,1)S(1)} %copy-done.9, f32[512,2048]{1,0:T(8,128)S(1)} %fusion.16), kind=kOutput, calls=%fused_computation.30 | convolution fusion | flops 2157445120 | bytes 9437184 | tf_op jit(solution)/shard_map/dot_general | solution.py:326
  36.4 0.0 copy-done.11
  36.4 0.0 copy-start.4
  36.4 0.1 collective-permute-start
  36.5 2.6 %collective-permute-done = bf16[512,1024]{1,0:T(8,128)(2,1)S(1)} collective-permute-done((bf16[512,1024]{1,0:T(8,128)(2,1)S(1)}, bf16[512,1024]{1,0:T(8,128)(2,1)S(1)}, u32[]{:S(2)}, u32[]{:S(2)}) %collective-permute-start) | collective-permute-done | bytes 1048608 | tf_op jit(solution)/shard_map/ppermute | solution.py:37
  39.2 0.0 copy-done.2
  39.2 0.5 fusion.18
  39.7 0.0 copy-start.10
  39.7 0.7 multiply_reduce_fusion.1
  40.4 0.0 copy-done.6
  40.4 0.6 fusion.14.left_ref
  41.0 0.0 copy-done.4
  41.0 0.0 copy-start.8
  41.0 1.0 copy-done.8
  42.0 0.0 copy-done.10
  42.0 3.8 %fusion.19.pred_ref = f32[512,1600]{1,0:T(8,128)} fusion(bf16[512,1024]{1,0:T(8,128)(2,1)S(1)} %fusion.14.left_ref, bf16[1024,1600]{0,1:T(8,128)(2,1)S(1)} %copy-done.10), kind=kOutput, calls=%fused_computation.44 | convolution fusion | flops 1677721600 | bytes 7602176 | tf_op jit(solution)/shard_map/dot_general | solution.py:333
  45.8 44.6 %all-to-all-done.1.block_ref = bf16[16,64,1600]{2,1,0:T(8,128)(2,1)} async-done(((bf16[16,64,1600]{2,1,0:T(8,128)(2,1)}), bf16[16,64,1600]{2,1,0:T(8,128)(2,1)}, u32[]{:S(2)}, u32[]{:S(2)}) %all-to-all-start.1) | async-done | bytes 3276832 | tf_op jit(solution)/shard_map/all_to_all | solution.py:332
  90.4 6.9 %shard_map.94.right_ref = bf16[512,1600]{1,0:T(8,128)(2,1)} custom-call(s32[8]{0:T(128)} %owner_ref.1, f32[512,1600]{1,0:T(8,128)} %fusion.19.pred_ref, bf16[16,64,1600]{2,1,0:T(8,128)(2,1)} %all-to-all-done.1.block_ref), custom_call_target="tpu_custom_call" | custom-call | flops 1638400 | bytes 6553600 | tf_op jit(solution)/shard_map/pallas_call | solution.py:264
  97.3 5.5 %convolution_convert_fusion.2 = bf16[512,1024]{1,0:T(8,128)(2,1)} fusion(bf16[512,1600]{1,0:T(8,128)(2,1)} %shard_map.94.right_ref, bf16[1024,1600]{0,1:T(8,128)(2,1)} %param.13), kind=kOutput, calls=%fused_computation.29 | convolution fusion | flops 1678245888 | bytes 5963776 | tf_op jit(solution)/shard_map/dot_general | solution.py:336
  102.8 0.0 collective-permute-start.1
  102.8 5.8 %shard_map.95 = bf16[1024,1600]{1,0:T(8,128)(2,1)} custom-call(bf16[512,1024]{1,0:T(8,128)(2,1)} %copy-done.8, bf16[512,1600]{1,0:T(8,128)(2,1)} %shard_map.94.right_ref), custom_call_target="tpu_custom_call" | custom-call | flops 1677721600 | bytes 5963776 | tf_op jit(solution)/shard_map/pallas_call | solution.py:292
  108.5 0.0 collective-permute-done.1
  108.6 3.7 %fusion.13 = (f32[512]{0:T(512)S(1)}, f32[512]{0:T(512)S(1)}) fusion(bf16[512,1024]{1,0:T(8,128)(2,1)} %collective-permute-done.1, bf16[512,1024]{1,0:T(8,128)(2,1)} %convolution_convert_fusion.2, f32[512]{0:T(512)S(1)} %add_rsqrt_fusion, f32[512]{0:T(512)S(1)} %broadcast_multiply_fusion.2, bf16[512,1024]{1,0:T(8,128)(2,1)} %copy-done.6, ...), kind=kLoop, calls=%fused_computation.27 | loop fusion | flops 6814720 | bytes 5251072 | tf_op jit(solution)/shard_map/reduce_sum | solution.py:340
  112.2 0.0 copy-done.3
  112.2 0.0 copy-done.5
  112.2 3.5 %multiply_convert_fusion.1 = bf16[512,1024]{1,0:T(8,128)(2,1)} fusion(bf16[512,1024]{1,0:T(8,128)(2,1)} %collective-permute-done.1, bf16[512,1024]{1,0:T(8,128)(2,1)} %convolution_convert_fusion.2, f32[512]{0:T(512)S(1)} %get-tuple-element.11, f32[512]{0:T(512)S(1)} %get-tuple-element.12, f32[512]{0:T(512)S(1)} %add_rsqrt_fusion, ...), kind=kLoop, calls=%fused_computation.22 | loop fusion | flops 7864320 | bytes 6299648 | tf_op jit(solution)/shard_map/convert_element_type | solution.py:343
  115.8 10.7 %convolution_convert_fusion = bf16[1024,2048]{1,0:T(8,128)(2,1)} fusion(bf16[512,1024]{1,0:T(8,128)(2,1)} %param.7, f32[512]{0:T(512)S(1)} %add_rsqrt_fusion.1, f32[512]{0:T(512)S(1)} %broadcast_multiply_fusion.3, f32[512,2048]{1,0:T(8,128)} %copy-done.11, bf16[512,1024]{1,0:T(8,128)(2,1)} %multiply_convert_fusion.1, bf16[2048,1024]{1,0:T(8,128)(2,1)} %param.12), kind=kOutput, calls=%fused_computation.13 | convolution fusion | flops 4319084544 | bytes 14684160 | tf_op jit(solution)/shard_map/dot_general | solution.py:347
  126.4 7.2 %convolution_convert_fusion.1 = bf16[1024,2048]{1,0:T(8,128)(2,1)} fusion(bf16[512,1024]{1,0:T(8,128)(2,1)} %multiply_convert_fusion.1, f32[512,2048]{1,0:T(8,128)} %copy-done.11), kind=kOutput, calls=%fused_computation.14 | convolution fusion | flops 2159017984 | bytes 9437184 | tf_op jit(solution)/shard_map/dot_general | solution.py:344
  133.7 121.4 %shard_map.96 = (f32[64,1600]{1,0:T(8,128)S(1)}, f32[64,2048]{1,0:T(8,128)S(1)}, f32[64,2048]{1,0:T(8,128)S(1)}) custom-call(bf16[4,2,2,64,1600]{4,3,2,1,0:T(8,128)(2,1)S(1)} %bitcast.23, bf16[4,2,2,64,2048]{4,3,2,1,0:T(8,128)(2,1)} %bitcast.26, bf16[4,2,2,64,2048]{4,3,2,1,0:T(8,128)(2,1)} %bitcast.25), custom_call_target="tpu_custom_call" | custom-call | tf_op jit(solution)/shard_map/pallas_call | solution.py:238
  255.1 0.8 copy.21
  255.9 0.8 copy.22
  256.7 0.8 copy.23
  (13 shorter events, 0.1 us)
Async XLA Ops:
  0.6 17.7 %copy-start = (bf16[16,64,1600]{2,1,0:T(8,128)(2,1)S(1)}, bf16[16,64,1600]{2,1,0:T(8,128)(2,1)}, u32[]{:S(2)}) copy-start(bf16[16,64,1600]{2,1,0:T(8,128)(2,1)} %param.10) | copy-start | bytes 9830404
  21.0 69.4 %all-to-all-start.1 = ((bf16[16,64,1600]{2,1,0:T(8,128)(2,1)}), bf16[16,64,1600]{2,1,0:T(8,128)(2,1)}, u32[]{:S(2)}, u32[]{:S(2)}) async-start(bf16[16,64,1600]{2,1,0:T(8,128)(2,1)} %gather_fusion), calls=%async_computation.1 | async-start | bytes 6815744 | tf_op jit(solution)/shard_map/all_to_all | solution.py:332
  28.6 5.1 %copy-start.9 = (bf16[2048,1024]{1,0:T(8,128)(2,1)S(1)}, bf16[2048,1024]{1,0:T(8,128)(2,1)}, u32[]{:S(2)}) copy-start(bf16[2048,1024]{1,0:T(8,128)(2,1)} %param.12) | copy-start | bytes 12582916
  33.7 2.7 %copy-start.11 = (f32[512,2048]{1,0:T(8,128)}, f32[512,2048]{1,0:T(8,128)S(1)}, u32[]{:S(2)}) copy-start(f32[512,2048]{1,0:T(8,128)S(1)} %fusion.16) | copy-start | bytes 12582916
  33.7 5.4 %copy-start.2 = (bf16[512,1024]{1,0:T(8,128)(2,1)S(1)}, bf16[512,1024]{1,0:T(8,128)(2,1)}, u32[]{:S(2)}) copy-start(bf16[512,1024]{1,0:T(8,128)(2,1)} %param.7) | copy-start | bytes 3145732
  36.4 4.5 %copy-start.4 = (bf16[512,1024]{1,0:T(8,128)(2,1)}, bf16[512,1024]{1,0:T(8,128)(2,1)S(1)}, u32[]{:S(2)}) copy-start(bf16[512,1024]{1,0:T(8,128)(2,1)S(1)} %convolution_convert_fusion.3) | copy-start | bytes 3145732
  36.4 2.7 %collective-permute-start = (bf16[512,1024]{1,0:T(8,128)(2,1)S(1)}, bf16[512,1024]{1,0:T(8,128)(2,1)S(1)}, u32[]{:S(2)}, u32[]{:S(2)}) collective-permute-start(bf16[512,1024]{1,0:T(8,128)(2,1)S(1)} %convolution_convert_fusion.3), channel_id=1, source_target_pairs={{0,1},{1,0},{2,3},{3,2},{4,5},{5,4},{6,7},{7,6},{8,9},{9,8},{10,11... | collective-permute-start | bytes 3145736 | tf_op jit(solution)/shard_map/ppermute | solution.py:37
  39.2 1.2 copy-start.6
  39.7 2.3 copy-start.10
  41.0 1.0 copy-start.8
  102.8 5.8 %collective-permute-start.1 = (bf16[512,1024]{1,0:T(8,128)(2,1)}, bf16[512,1024]{1,0:T(8,128)(2,1)}, u32[]{:S(2)}, u32[]{:S(2)}) collective-permute-start(bf16[512,1024]{1,0:T(8,128)(2,1)} %convolution_convert_fusion.2), channel_id=1, source_target_pairs={{0,1},{1,0},{2,3},{3,2},{4,5},{5,4},{6,7},{7,6},{8,9},{9,8},{10,11... | collective-permute-start | bytes 3145736 | tf_op jit(solution)/shard_map/ppermute | solution.py:37
  108.5 3.7 %copy-start.3 = (bf16[512,1024]{1,0:T(8,128)(2,1)S(1)}, bf16[512,1024]{1,0:T(8,128)(2,1)}, u32[]{:S(2)}) copy-start(bf16[512,1024]{1,0:T(8,128)(2,1)} %param.7) | copy-start | bytes 3145732
  108.5 3.7 %copy-start.5 = (bf16[512,1024]{1,0:T(8,128)(2,1)S(1)}, bf16[512,1024]{1,0:T(8,128)(2,1)}, u32[]{:S(2)}) copy-start(bf16[512,1024]{1,0:T(8,128)(2,1)} %copy-done.4) | copy-start | bytes 3145732
  108.5 3.7 %copy-start.7 = (bf16[512,1024]{1,0:T(8,128)(2,1)S(1)}, bf16[512,1024]{1,0:T(8,128)(2,1)}, u32[]{:S(2)}) copy-start(bf16[512,1024]{1,0:T(8,128)(2,1)} %copy-done.6) | copy-start | bytes 3145732
  126.4 7.2 %copy-start.1 = (bf16[1024,1600]{1,0:T(8,128)(2,1)S(1)}, bf16[1024,1600]{1,0:T(8,128)(2,1)}, u32[]{:S(2)}) copy-start(bf16[1024,1600]{1,0:T(8,128)(2,1)} %shard_map.95) | copy-start | bytes 9830404
